TPU v7x, 32 devices: a whole 2x2x4 slice. The times are simulated.
32 devices in a mesh: dp: 16 (over z, x, core), tensor: 2 (over y).
Axes of the slice: x: 2, y: 2, z: 4, core: 2. Of those that a mesh axis runs over, the one named last changes fastest.
Arguments:
- tokens: bfloat16 [4096, 1024], P(('dp', 'tensor')), may hold values from -6 to 6
- seq_lens: int32 [16, 8], P('dp'), may hold values from 0 to 256, as said below
- g_attn: bfloat16 [1024], P('dp'), may hold values from 0.5 to 1.5
- w_qkv: bfloat16 [1024, 3, 1024], P('dp', None, 'tensor'), may hold values from -0.1875 to 0.1875
- w_ao: bfloat16 [1024, 1024], P('tensor', 'dp'), may hold values from -0.75 to 0.75
- g_mlp: bfloat16 [1024], P('dp'), may hold values from 0.5 to 1.5
- w_in: bfloat16 [1024, 2, 2624], P('dp', None, 'tensor'), may hold values from -0.1875 to 0.1875
- w_mo: bfloat16 [2624, 1024], P('tensor', 'dp'), may hold values from -0.15625 to 0.15625
- cotangent: bfloat16 [4096, 1024], P(('dp', 'tensor')), may hold values from -6 to 6
Outputs:
- output: bfloat16 [4096, 1024], P(('dp', 'tensor'))
- grad_input: float32 [4096, 1024], P(('dp', 'tensor'))
- grad_g_attn: float32 [1024], P(('dp', 'tensor'))
- grad_qkv: float32 [1024, 3, 1024], P('dp', None, 'tensor')
- grad_ao: float32 [1024, 1024], P('tensor', 'dp')
- grad_g_mlp: float32 [1024], P(('dp', 'tensor'))
- grad_in: float32 [1024, 2, 2624], P('dp', None, 'tensor')
- grad_mo: float32 [2624, 1024], P('tensor', 'dp')
Inputs may be any that keep to these rules, and one draw needn't show every extreme that they name: `seq_lens`: A group's lengths sum to at most 256; a length of 0 is an empty slot; in every draw some group holds one sequence of 256 tokens.
All inputs are finite; a program needn't handle non-finite values.
Results may differ from a plain program's by a relative error of at most 0.014.
Values may be sent and summed in bfloat16 or wider, within the bound.
No kernel may reach another device: no remote copies, remote signals or barrier semaphores. Data moves between devices by JAX's collectives and lax.ppermute only.
A program may use at most 128 MiB of HBM per device.

v0:
```python
import math

import jax
import jax.numpy as jnp
from jax import lax
from jax.experimental import pallas as pl
from jax.experimental.pallas import tpu as pltpu
from jax.sharding import PartitionSpec as P

HDIM = 64
ROPE_BASE = 160000.0
BF = jnp.bfloat16
F32 = jnp.float32


def layout(lengths, index):
    ends = jnp.cumsum(lengths)
    passed = ends[None, :] <= index[:, None]
    doc_ids = jnp.sum(passed.astype(jnp.int32), axis=1)
    begins = jnp.max(jnp.where(passed, ends[None, :], jnp.zeros_like(ends)[None, :]), axis=1)
    return (doc_ids, index - begins)


def tables(positions, lanes):
    half = HDIM // 2
    lane = jnp.arange(lanes, dtype=jnp.int32)
    rates = jnp.exp((lane % half).astype(F32) * (-2.0 * math.log(ROPE_BASE) / HDIM))
    angles = positions.astype(F32)[:, None] * rates[None, :]
    sign = jnp.where(lane % HDIM < half, -1.0, 1.0)
    return jnp.cos(angles), jnp.sin(angles) * sign[None, :]


def normalize(values):
    center = values - jnp.mean(values, axis=-1, keepdims=True)
    factor = lax.rsqrt(jnp.mean(center * center, axis=-1, keepdims=True) + 1e-05)
    return (center * factor, factor)


def norm_back(grad_hat, normed, factor):
    return factor * (
        grad_hat
        - jnp.mean(grad_hat, axis=-1, keepdims=True)
        - normed * jnp.mean(grad_hat * normed, axis=-1, keepdims=True)
    )


def ein(spec, left, right):
    return jnp.einsum(spec, left, right, preferred_element_type=F32)


def nn(left, right):
    return jnp.dot(left, right, preferred_element_type=F32)


def nt(left, right):
    return lax.dot_general(left, right, (((1,), (1,)), ((), ())), preferred_element_type=F32)


def tn(left, right):
    return lax.dot_general(left, right, (((0,), (0,)), ((), ())), preferred_element_type=F32)


def shape(dims, kind):
    return jax.ShapeDtypeStruct(dims, kind)


ANYWHERE = pl.BlockSpec(memory_space=pl.ANY)
WHOLE = pl.BlockSpec(memory_space=pltpu.VMEM)


def load_planes(own_hbm, oth_hbm, own, oth, sems):
    copies = []
    for plane in range(own.shape[0]):
        pair = (
            pltpu.make_async_copy(own_hbm.at[plane], own.at[plane], sems.at[0, plane]),
            pltpu.make_async_copy(oth_hbm.at[plane], oth.at[plane], sems.at[1, plane]),
        )
        copies.append(pair)
    return copies


def begin(copies, order):
    for plane in order:
        copies[plane][0].start()
        copies[plane][1].start()


def finish(copies, plane):
    copies[plane][0].wait()
    copies[plane][1].wait()


def planes_scratch(block):
    return [
        pltpu.VMEM(block, BF),
        pltpu.VMEM(block, BF),
        pltpu.SemaphoreType.DMA((2, block[0])),
    ]


def swing(values, cosine, sine):
    lanes = values.shape[-1]
    half = HDIM // 2
    lane = lax.broadcasted_iota(jnp.int32, values.shape, 1)
    turned = jnp.where(
        lane % HDIM < half,
        pltpu.roll(values, lanes - half, 1),
        pltpu.roll(values, half, 1),
    )
    return values * cosine + turned * sine


def head_probs(query, key, same):
    scores = jnp.where(same, nt(query, key) * 0.125, -1e30)
    peak = jnp.max(scores, axis=-1, keepdims=True)
    raised = jnp.exp(scores - peak)
    return raised * (1.0 / jnp.sum(raised, axis=-1, keepdims=True))


def attend_kernel(x, own_hbm, oth_hbm, docs, docs_row, cos, sin, qkv, mixed, hat, part, away, own, oth, sems):
    copies = load_planes(own_hbm, oth_hbm, own, oth, sems)
    begin(copies, range(4))
    normed, _ = normalize(x[...].astype(F32))
    hat[...] = normed.astype(BF)
    cut = own.shape[1]
    count = part.shape[0]
    for plane in range(3):
        finish(copies, plane)
        value = nn(hat[:, :cut], own[plane]) + nn(hat[:, cut:], oth[plane])
        if plane < 2:
            value = swing(value, cos[...], sin[...])
        qkv[plane] = value.astype(BF)
    same = docs[...] == docs_row[...]
    for head in range(qkv.shape[2] // HDIM):
        at = slice(head * HDIM, (head + 1) * HDIM)
        probs = head_probs(qkv[0, :, at], qkv[1, :, at], same)
        mixed[:, at] = nn(probs.astype(BF), qkv[2, :, at]).astype(BF)
    finish(copies, 3)
    for weights, lo in ((own, 0), (oth, cut)):
        full = nt(mixed[...], weights[3])
        part[:, lo : lo + cut] = full[:count]
        away[:, lo : lo + cut] = full[count:].astype(BF)


def attend_call(x, own, oth, docs, cos, sin):
    group, width = x.shape
    planes, cut, lanes = own.shape
    return pl.pallas_call(
        attend_kernel,
        out_shape=(
            shape((3, group, lanes), BF),
            shape((group, lanes), BF),
            shape((group, width), BF),
            shape((group // 2, width), F32),
            shape((group // 2, width), BF),
        ),
        in_specs=[WHOLE, ANYWHERE, ANYWHERE, WHOLE, WHOLE, WHOLE, WHOLE],
        out_specs=(WHOLE,) * 5,
        scratch_shapes=planes_scratch(own.shape),
        name="attend",
    )(x, own, oth, docs[:, None], docs[None, :], cos, sin)


def mlp_kernel(hat, cot, own_hbm, oth_hbm, three, part, away, out_part, out_away, own, oth, sems, gate, upper, back):
    copies = load_planes(own_hbm, oth_hbm, own, oth, sems)
    begin(copies, range(3))
    cut = own.shape[1]
    count = part.shape[0]
    finish(copies, 0)
    gate[...] = nn(hat[:, :cut], own[0]) + nn(hat[:, cut:], oth[0])
    finish(copies, 1)
    upper[...] = nn(hat[:, :cut], own[1]) + nn(hat[:, cut:], oth[1])
    finish(copies, 2)
    back[...] = nn(cot[:, :cut], own[2]) + nn(cot[:, cut:], oth[2])
    step = 16

    def chunk(i, carry):
        at = pl.ds(pl.multiple_of(i * step, step), step)
        v, u, g = gate[at, :], upper[at, :], back[at, :]
        share = 0.5 * (1.0 + lax.erf(v * (1.0 / math.sqrt(2.0))))
        slope = share + v * (jnp.exp(-0.5 * v * v) * (1.0 / math.sqrt(2.0 * math.pi)))
        active = v * share
        three[0, at, :] = (g * u * slope).astype(BF)
        three[1, at, :] = (g * active).astype(BF)
        three[2, at, :] = (active * u).astype(BF)
        return carry

    lax.fori_loop(0, gate.shape[0] // step, chunk, 0)
    for weights, lo in ((own, 0), (oth, cut)):
        full = nt(three[0], weights[0]) + nt(three[1], weights[1])
        part[:, lo : lo + cut] = full[:count]
        away[:, lo : lo + cut] = full[count:].astype(BF)
        full = nt(three[2], weights[2])
        out_part[:, lo : lo + cut] = full[:count]
        out_away[:, lo : lo + cut] = full[count:].astype(BF)


def mlp_call(hat, cot, own, oth):
    group, width = hat.shape
    hidden = own.shape[2]
    half = group // 2
    return pl.pallas_call(
        mlp_kernel,
        out_shape=(
            shape((3, group, hidden), BF),
            shape((half, width), F32),
            shape((half, width), BF),
            shape((half, width), F32),
            shape((half, width), BF),
        ),
        in_specs=[WHOLE, WHOLE, ANYWHERE, ANYWHERE],
        out_specs=(WHOLE,) * 5,
        scratch_shapes=planes_scratch(own.shape) + [pltpu.VMEM((group, hidden), F32)] * 3,
        name="mlp",
    )(hat, cot, own, oth)


def back_kernel(grad, qkv, own_hbm, oth_hbm, docs, docs_row, cos, sin, three, part, away, own, oth, sems, gmix, wide):
    copies = load_planes(own_hbm, oth_hbm, own, oth, sems)
    begin(copies, (3, 0, 1, 2))
    cut = own.shape[1]
    count = part.shape[0]
    finish(copies, 3)
    gmix[...] = (nn(grad[:, :cut], own[3]) + nn(grad[:, cut:], oth[3])).astype(BF)
    same = docs[...] == docs_row[...]
    for head in range(qkv.shape[2] // HDIM):
        at = slice(head * HDIM, (head + 1) * HDIM)
        query, key, value, outer = qkv[0, :, at], qkv[1, :, at], qkv[2, :, at], gmix[:, at]
        probs = head_probs(query, key, same)
        three[2, :, at] = tn(probs.astype(BF), outer).astype(BF)
        grad_probs = nt(outer, value)
        inner = jnp.sum(probs * grad_probs, axis=-1, keepdims=True)
        grad_scores = (probs * (grad_probs - inner) * 0.125).astype(BF)
        wide[0, :, at] = nn(grad_scores, key)
        wide[1, :, at] = tn(grad_scores, query)
    for plane in range(2):
        three[plane] = swing(wide[plane], cos[...], -sin[...]).astype(BF)
    for plane in range(3):
        finish(copies, plane)
    for weights, lo in ((own, 0), (oth, cut)):
        full = nt(three[0], weights[0]) + nt(three[1], weights[1]) + nt(three[2], weights[2])
        part[:, lo : lo + cut] = full[:count]
        away[:, lo : lo + cut] = full[count:].astype(BF)


def back_call(grad, qkv, own, oth, docs, cos, sin):
    group, width = grad.shape
    lanes = own.shape[2]
    return pl.pallas_call(
        back_kernel,
        out_shape=(
            shape((3, group, lanes), BF),
            shape((group // 2, width), F32),
            shape((group // 2, width), BF),
        ),
        in_specs=[WHOLE, WHOLE, ANYWHERE, ANYWHERE, WHOLE, WHOLE, WHOLE, WHOLE],
        out_specs=(WHOLE,) * 3,
        scratch_shapes=planes_scratch(own.shape)
        + [pltpu.VMEM((group, lanes), BF), pltpu.VMEM((2, group, lanes), F32)],
        name="attend_back",
    )(grad, qkv, own, oth, docs[:, None], docs[None, :], cos, sin)


def outer_kernel(first, second, three, last, out):
    plane = pl.program_id(0)
    split = pl.num_programs(0) - 1

    @pl.when(plane < split)
    def _():
        out[0] = tn(first[...], three[0]).astype(BF)

    @pl.when(plane == split)
    def _():
        out[0] = tn(second[...], last[...]).astype(BF)


def weight_grads(first, second, three, last, side):
    group, width = first.shape
    cut = width // 2
    lanes = three.shape[2]
    merged = last is None
    planes = 3 if merged else 4
    last_spec = pl.BlockSpec((group, lanes), lambda i: (0, 0))
    if merged:
        last = three
        last_spec = pl.BlockSpec((None, group, lanes), lambda i: (2, 0, 0))
    return pl.pallas_call(
        outer_kernel,
        grid=(planes,),
        out_shape=shape((planes, cut, lanes), BF),
        in_specs=[
            pl.BlockSpec((group, cut), lambda i: (0, side)),
            pl.BlockSpec((group, cut), lambda i: (0, side)),
            pl.BlockSpec((1, group, lanes), lambda i: (jnp.minimum(i, planes - 2), 0, 0)),
            last_spec,
        ],
        out_specs=pl.BlockSpec((1, cut, lanes), lambda i: (i, 0, 0)),
        name="weight_grads",
    )(first, second, three, last)


def first_kernel(own, theirs, down, up):
    total = (own[...].astype(F32) + theirs[...].astype(F32)).astype(BF)
    h = total.shape[1] // 2
    down[...] = total[:, :h]
    up[...] = total[:, h:]


def first_call(own, theirs, rows, j):
    planes, _, lanes = own.shape
    block = pl.BlockSpec((1, rows, lanes), lambda i: (i, j, 0))
    out = pl.BlockSpec((1, rows // 2, lanes), lambda i: (i, 0, 0))
    return pl.pallas_call(
        first_kernel,
        grid=(planes,),
        out_shape=(shape((planes, rows // 2, lanes), BF),) * 2,
        in_specs=[block, block],
        out_specs=(out, out),
        name="ring_first",
    )(own, theirs)


def middle_kernel(own_a, theirs_a, own_b, theirs_b, down, up, out_a, out_b):
    a = own_a[...].astype(F32) + theirs_a[...].astype(F32)
    b = own_b[...].astype(F32) + theirs_b[...].astype(F32)
    rows = a.shape[1]
    h = down.shape[1]
    if h == rows:
        out_a[...] = (a + down[...].astype(F32)).astype(BF)
        out_b[...] = (b + up[...].astype(F32)).astype(BF)
    else:
        out_a[:, :h] = (a[:, :h] + down[...].astype(F32)).astype(BF)
        out_a[:, h:] = a[:, h:].astype(BF)
        out_b[:, :h] = b[:, :h].astype(BF)
        out_b[:, h:] = (b[:, h:] + up[...].astype(F32)).astype(BF)


def middle_call(own, theirs, down, up, rows, j):
    planes, _, lanes = own.shape
    left = pl.BlockSpec((1, rows, lanes), lambda i: (i, j, 0))
    right = pl.BlockSpec((1, rows, lanes), lambda i: (i, j + 1, 0))
    got = pl.BlockSpec((1, down.shape[1], lanes), lambda i: (i, 0, 0))
    out = pl.BlockSpec((1, rows, lanes), lambda i: (i, 0, 0))
    return pl.pallas_call(
        middle_kernel,
        grid=(planes,),
        out_shape=(shape((planes, rows, lanes), BF),) * 2,
        in_specs=[left, left, right, right, got, got],
        out_specs=(out, out),
        name="ring_middle",
    )(own, theirs, own, theirs, down, up)


def last_kernel(own, theirs, down, up, out):
    out[...] = (own[...].astype(F32) + theirs[...].astype(F32)) + (
        down[...].astype(F32) + up[...].astype(F32)
    )


def last_call(own, theirs, down, up, rows):
    planes, _, lanes = own.shape
    block = pl.BlockSpec((1, rows, lanes), lambda i: (i, 0, 0))
    return pl.pallas_call(
        last_kernel,
        grid=(planes,),
        out_shape=shape((planes, rows, lanes), F32),
        in_specs=[block] * 4,
        out_specs=block,
        name="ring_last",
    )(own, theirs, down, up)


def tie(value, *after):
    return lax.optimization_barrier((value, after))[0]


class Ring:
    def __init__(self, size):
        self.size = size
        self.chips = size // 2
        self.ringed = self.chips % 2 == 0 and 4 <= self.chips <= 16
        half = self.chips // 2
        order = [2 * p for p in range(half)] + [2 * (self.chips - 1 - p) + 1 for p in range(half, self.chips)]
        self.forward = self.pairs(order, 1)
        self.backward = self.pairs(order, -1)
        self.core = [(i, i ^ 1) for i in range(size)]
        self.groups = [[i for i in range(size) if i % 2 == c] for c in range(2)]

    def pairs(self, order, step):
        n = self.chips
        return [
            (2 * order[k] + c, 2 * order[(k + step) % n] + c) for k in range(n) for c in range(2)
        ]

    def arrival(self, rows):
        me = lax.axis_index("dp")
        chip, core = me // 2, me % 2
        n, half = self.chips, self.chips // 2
        place = jnp.arange(self.size * rows, dtype=jnp.int32)
        other = place // (n * rows)
        block = (place // rows) % n
        if self.ringed:
            spot = jnp.where(chip % 2 == 0, chip // 2, n - 1 - chip // 2)
            offset = jnp.where(block % 2 == 1, -((block + 1) // 2), block // 2)
            where_at = (spot + offset + n) % n
            source = jnp.where(where_at < half, 2 * where_at, 2 * (n - 1 - where_at) + 1)
        else:
            source = block
        return (source * 2 + (core + other) % 2) * rows + place % rows

    def ahead(self, block):
        return lax.ppermute(block, "dp", self.forward)

    def back(self, block):
        return lax.ppermute(block, "dp", self.backward)

    def across(self, block):
        return lax.ppermute(block, "dp", self.core)


class Gather:
    def __init__(self, ring, block):
        self.ring = ring
        self.block = block
        self.pieces = [block]
        self.a = self.b = block
        self.left = ring.chips // 2 if ring.ringed else 0

    def step(self, *after):
        if self.left == 0:
            return
        a, b = (tie((self.a, self.b), *after) if after else (self.a, self.b))
        self.left -= 1
        if self.left == 0:
            rows = a.shape[1]
            a, b = a[:, : rows // 2], b[:, rows // 2 :]
        self.a, self.b = self.ring.ahead(a), self.ring.back(b)
        self.pieces += [self.a, self.b]

    def done(self):
        if self.ring.ringed:
            own = jnp.concatenate(self.pieces, axis=1)
        else:
            own = lax.all_gather(
                self.block, "dp", axis=1, tiled=True, axis_index_groups=self.ring.groups
            )
        return own, self.ring.across(own)


class Reduce:
    def __init__(self, ring, own, theirs):
        self.ring, self.own, self.theirs = ring, own, theirs
        self.rows = own.shape[1] // ring.chips
        self.left = ring.chips // 2 if ring.ringed else 0
        self.down = self.up = None
        self.sent = ()

    def step(self, *after):
        if self.left == 0:
            return
        j = 2 * self.left - 1
        if self.down is None:
            down, up = first_call(self.own, self.theirs, self.rows, j)
        else:
            down, up = middle_call(self.own, self.theirs, self.down, self.up, self.rows, j)
        if after:
            down, up = tie((down, up), *after)
        self.left -= 1
        self.sent = (down, up)
        self.down, self.up = self.ring.back(down), self.ring.ahead(up)

    def done(self, *after):
        if not self.ring.ringed:
            total = self.own.astype(F32) + self.theirs.astype(F32)
            return lax.psum_scatter(
                total, "dp", scatter_dimension=1, tiled=True, axis_index_groups=self.ring.groups
            )
        own = tie(self.own, *after) if after else self.own
        return last_call(own, self.theirs, self.down, self.up, self.rows)


def swap(block):
    return lax.ppermute(block, "tensor", [(0, 1), (1, 0)])


def body(tokens, seq_lens, g_attn, w_qkv, w_ao, g_mlp, w_in, w_mo, cotangent):
    ring = Ring(lax.axis_size("dp"))
    rows = w_qkv.shape[0]
    count = tokens.shape[0]
    side = lax.axis_index("tensor")
    group = 2 * count
    width = tokens.shape[1]

    gain_one = g_attn.astype(F32)
    gain_two = g_mlp.astype(F32)
    plain_qkv = jnp.transpose(w_qkv, (1, 0, 2)).astype(F32)
    plain_in = jnp.transpose(w_in, (1, 0, 2)).astype(F32)
    block_a = jnp.concatenate(
        [(plain_qkv * gain_one[None, :, None]).astype(BF), w_ao.T[None]], axis=0
    )
    hidden = w_in.shape[2]
    block_b = jnp.concatenate(
        [(plain_in * gain_two[None, :, None]).astype(BF), w_mo.T[None]], axis=0
    )
    block_b = jnp.pad(block_b, ((0, 0), (0, 0), (0, -hidden % 128)))
    gather_a = Gather(ring, block_a)
    gather_a.step()
    gather_b = Gather(ring, tie(block_b, block_a))
    gather_b.step()

    index = (jnp.arange(group, dtype=jnp.int32) + side * count) % group
    docs, positions = layout(seq_lens[0], index)
    cosine, sine = tables(positions, w_qkv.shape[2])

    places = ring.arrival(rows)
    chosen = (jnp.arange(width, dtype=jnp.int32)[:, None] == places[None, :]).astype(BF)
    moved = ein("td,de->te", jnp.concatenate([tokens, cotangent], axis=0), chosen).astype(BF)
    moved_other = swap(moved)
    tokens_all = jnp.concatenate([moved[:count], moved_other[:count]], axis=0)
    cot_all = jnp.concatenate([moved[count:], moved_other[count:]], axis=0)

    gather_a.step(moved)
    gather_a.step(cosine, sine)
    gather_b.step(*gather_a.pieces[3:5])
    gather_a.step(tokens_all, cot_all)
    own_a, oth_a = gather_a.done()

    normed_one, factor_one = normalize(moved[:count].astype(F32))
    qkv, mixed, hat_one, part, away = attend_call(tokens_all, own_a, oth_a, docs, cosine, sine)
    swapped = swap(away)
    gather_b.step(away)
    residual = moved[:count].astype(F32) + part + swapped.astype(F32)
    normed_two, factor_two = normalize(residual)
    hat_own = normed_two.astype(BF)
    hat_two = jnp.concatenate([hat_own, swap(hat_own)], axis=0)
    gather_b.step(hat_own)
    own_b, oth_b = gather_b.done()

    three_b, part, away, out_part, out_away = mlp_call(hat_two, cot_all, own_b, oth_b)
    swapped = swap(away)
    side_b = weight_grads(hat_two, cot_all, three_b, None, 1)
    cross_b = ring.across(side_b)
    main_b = weight_grads(tie(hat_two, side_b), cot_all, three_b, None, 0)
    reduce_b = Reduce(ring, main_b, cross_b)
    reduce_b.step()
    grad_hat_two = part + tie(swapped, *reduce_b.sent).astype(F32)
    grad_residual = moved[count:].astype(F32) + norm_back(grad_hat_two, normed_two, factor_two)
    grad_res_own = grad_residual.astype(BF)
    grad_res_all = jnp.concatenate([grad_res_own, swap(grad_res_own)], axis=0)
    reduce_b.step(grad_res_own)
    three_a, part, away = back_call(
        tie(grad_res_all, *reduce_b.sent), qkv, own_a, oth_a, docs, cosine, sine
    )
    reduce_b.step(away)
    swapped = swap(away)
    side_a = weight_grads(tie(hat_one, *reduce_b.sent), grad_res_all, three_a, mixed, 1)
    cross_a = ring.across(side_a)
    main_a = weight_grads(tie(hat_one, side_a), grad_res_all, three_a, mixed, 0)
    reduce_a = Reduce(ring, main_a, cross_a)
    reduce_a.step()
    reduce_b.step(*reduce_a.sent)
    reduce_a.step(*reduce_b.sent)
    raw_b = reduce_b.done(*reduce_a.sent)

    grad_hat_one = part + tie(swapped, *reduce_a.sent).astype(F32)
    grad_input = grad_residual + norm_back(grad_hat_one, normed_one, factor_one)
    top = lax.reduce_precision(grad_input, 8, 7)
    middle = lax.reduce_precision(grad_input - top, 8, 7)
    parts = jnp.concatenate([top, middle, grad_input - top - middle], axis=0).astype(BF)
    spread = ein("te,de->td", parts, chosen)
    grad_input = spread[:count] + spread[count : 2 * count] + spread[2 * count :]
    out_swapped = swap(tie(out_away, swapped))
    reduce_a.step(grad_input)

    raw_b = tie(raw_b, *reduce_a.sent)[:, :, :hidden]
    grad_in = jnp.transpose(raw_b[:2] * gain_two[None, :, None], (1, 0, 2))
    grad_mo = raw_b[2].T
    gain_two_sum = jnp.sum(plain_in * raw_b[:2], axis=(0, 2))
    reduce_a.step(grad_in, grad_mo, gain_two_sum)
    output = (residual + out_part + tie(out_swapped, *reduce_a.sent).astype(F32)).astype(BF)
    output = ein("te,de->td", output, chosen).astype(BF)
    raw_a = reduce_a.done()

    gain_sums = jnp.stack(
        [jnp.sum(plain_qkv * raw_a[:3], axis=(0, 2)), gain_two_sum]
    )
    share = rows // 2
    gain_shares = lax.dynamic_slice_in_dim(gain_sums, side * share, share, 1) + swap(
        lax.dynamic_slice_in_dim(gain_sums, (1 - side) * share, share, 1)
    )
    return (
        output,
        grad_input,
        gain_shares[0],
        jnp.transpose(raw_a[:3] * gain_one[None, :, None], (1, 0, 2)),
        raw_a[3].T,
        gain_shares[1],
        grad_in,
        grad_mo,
    )


def solution(mesh):
    return jax.shard_map(
        body,
        mesh=mesh,
        in_specs=(
            P(("dp", "tensor"), None),
            P("dp", None),
            P("dp"),
            P("dp", None, "tensor"),
            P("tensor", "dp"),
            P("dp"),
            P("dp", None, "tensor"),
            P("tensor", "dp"),
            P(("dp", "tensor"), None),
        ),
        out_specs=(
            P(("dp", "tensor"), None),
            P(("dp", "tensor"), None),
            P(("dp", "tensor")),
            P("dp", None, "tensor"),
            P("tensor", "dp"),
            P(("dp", "tensor")),
            P("dp", None, "tensor"),
            P("tensor", "dp"),
        ),
        check_vma=False,
    )
```

profile of v0, /device:TPU:0, one launch (start us, length us, event | category | flops | bytes accessed | tf_op | source)
XLA Modules:
  0.0 252.9 jit_solution(14124483323935391902)
XLA Ops:
  3.2 3.1 %collective-permute-start.1 = (bf16[4,64,512]{2,1,0:T(8,128)(2,1)S(1)}, bf16[4,64,512]{2,1,0:T(8,128)(2,1)S(1)}, u32[]{:S(2)}, u32[]{:S(2)}) collective-permute-start(bf16[4,64,512]{2,1,0:T(8,128)(2,1)S(1)} %get-tuple-element.183), channel_id=1, source_target_pairs={{0,8},{2,10},{8,16},{10,18},{16,24},{18,26},{24,28},{26,30},{28,20... | collective-permute-start | bytes 786440 | tf_op jit(solution)/shard_map/ppermute | solution.py:412
  6.3 2.0 fusion.6
  8.4 2.0 collective-permute-start
  10.7 2.8 %fusion.27 = (f32[256,512]{1,0:T(8,128)}, f32[256,512]{1,0:T(8,128)}) fusion(f32[512]{0:T(512)S(1)} %get-tuple-element.192, f32[512]{0:T(512)S(1)} %get-tuple-element.191, f32[256]{0:T(256)S(1)} %subtract_convert_fusion), kind=kLoop, calls=%fused_computation.41 | loop fusion | flops 262144 | bytes 1053696 | tf_op jit(solution)/shard_map/mul | solution.py:30
  17.2 3.8 %collective-permute-done.3 = bf16[4,64,512]{2,1,0:T(8,128)(2,1)S(1)} collective-permute-done((bf16[4,64,512]{2,1,0:T(8,128)(2,1)S(1)}, bf16[4,64,512]{2,1,0:T(8,128)(2,1)S(1)}, u32[]{:S(2)}, u32[]{:S(2)}) %collective-permute-start.3) | collective-permute-done | bytes 262176 | tf_op jit(solution)/shard_map/ppermute | solution.py:412
  26.8 2.1 collective-permute-done.5
  32.7 2.8 %collective-permute-done.7 = bf16[4,32,512]{2,1,0:T(8,128)(2,1)S(1)} collective-permute-done((bf16[4,32,512]{2,1,0:T(8,128)(2,1)S(1)}, bf16[4,32,512]{2,1,0:T(8,128)(2,1)S(1)}, u32[]{:S(2)}, u32[]{:S(2)}) %collective-permute-start.7) | collective-permute-done | bytes 131104 | tf_op jit(solution)/shard_map/ppermute | solution.py:412
  40.5 11.8 %collective-permute-done.12 = bf16[3,64,1408]{2,1,0:T(8,128)(2,1)} collective-permute-done((bf16[3,64,1408]{2,1,0:T(8,128)(2,1)S(1)}, bf16[3,64,1408]{2,1,0:T(8,128)(2,1)}, u32[]{:S(2)}, u32[]{:S(2)}) %collective-permute-start.12) | collective-permute-done | bytes 540704 | tf_op jit(solution)/shard_map/ppermute | solution.py:412
  61.1 7.9 %attend.1 = (bf16[3,256,512]{2,1,0:T(8,128)(2,1)}, bf16[256,512]{1,0:T(8,128)(2,1)}, bf16[256,1024]{1,0:T(8,128)(2,1)}, f32[128,1024]{1,0:T(8,128)}, bf16[128,1024]{1,0:T(8,128)(2,1)}) custom-call(bf16[256,1024]{1,0:T(8,128)(2,1)} %get-tuple-element.189.x, bf16[4,512,512]{2,1,0:T(8,128)(2,1)} %copy-done.1, ...), custom_call_target="tpu_custom_call" | custom-call | tf_op jit(solution)/shard_map/attend/pallas_call | solution.py:148
  76.9 10.1 %collective-permute-done.16 = bf16[3,64,1408]{2,1,0:T(8,128)(2,1)S(1)} collective-permute-done((bf16[3,64,1408]{2,1,0:T(8,128)(2,1)}, bf16[3,64,1408]{2,1,0:T(8,128)(2,1)S(1)}, u32[]{:S(2)}, u32[]{:S(2)}) %collective-permute-start.16) | collective-permute-done | bytes 540704 | tf_op jit(solution)/shard_map/ppermute | solution.py:412
  91.3 2.5 collective-permute-done.18
  96.3 7.7 %collective-permute-done.11 = bf16[128,1024]{1,0:T(8,128)(2,1)S(1)} collective-permute-done((bf16[128,1024]{1,0:T(8,128)(2,1)S(1)}, bf16[128,1024]{1,0:T(8,128)(2,1)S(1)}, u32[]{:S(2)}, u32[]{:S(2)}) %collective-permute-start.11) | collective-permute-done | bytes 262176 | tf_op jit(solution)/shard_map/ppermute | solution.py:483
  104.8 10.4 %mlp.1 = (bf16[3,256,1408]{2,1,0:T(8,128)(2,1)}, f32[128,1024]{1,0:T(8,128)}, bf16[128,1024]{1,0:T(8,128)(2,1)}, f32[128,1024]{1,0:T(8,128)}, bf16[128,1024]{1,0:T(8,128)(2,1)}) custom-call(bf16[256,1024]{1,0:T(8,128)(2,1)} %pad_maximum_fusion.2.hat.first, bf16[256,1024]{1,0:T(8,128)(2,1)} %get-tuple-element.190.cot.second, ...), custom_call_target="tpu_custom_call" | custom-call | tf_op jit(solution)/shard_map/mlp/pallas_call | solution.py:202
  115.2 5.0 %weight_grads.4 = bf16[3,512,1408]{2,1,0:T(8,128)(2,1)} custom-call(bf16[256,1024]{1,0:T(8,128)(2,1)} %pad_maximum_fusion.2.hat.first, bf16[256,1024]{1,0:T(8,128)(2,1)} %get-tuple-element.190.cot.second, bf16[3,256,1408]{2,1,0:T(8,128)(2,1)} %get-tuple-element.91.three.last, bf16[3,256,1408]{2,1,0:T(8,128)(2,1)} %get-tuple-element.91.three.last), custom_call_target="tpu_custom_call" | custom-call | tf_op jit(solution)/shard_map/weight_grads/pallas_call | solution.py:287
  121.3 5.0 %weight_grads.5.own.own_a.own_b = bf16[3,512,1408]{2,1,0:T(8,128)(2,1)} custom-call(bf16[256,1024]{1,0:T(8,128)(2,1)} %pad_maximum_fusion.2.hat.first, bf16[256,1024]{1,0:T(8,128)(2,1)} %get-tuple-element.190.cot.second, bf16[3,256,1408]{2,1,0:T(8,128)(2,1)} %get-tuple-element.91.three.last, bf16[3,256,1408]{2,1,0:T(8,128)(2,1)} %get-tuple-element.91.three.last), custom_call_target="tpu_custom_call" | custom-call | tf_op jit(solution)/shard_map/weight_grads/pallas_call | solution.py:287
  127.9 2.9 %ring_first.2 = (bf16[3,32,1408]{2,1,0:T(8,128)(2,1)}, bf16[3,32,1408]{2,1,0:T(8,128)(2,1)}) custom-call(bf16[3,512,1408]{2,1,0:T(8,128)(2,1)} %weight_grads.5.own.own_a.own_b, bf16[3,512,1408]{2,1,0:T(8,128)(2,1)} %collective-permute-done.22.theirs.theirs_a.theirs_b), custom_call_target="tpu_custom_call" | custom-call | tf_op jit(solution)/shard_map/ring_first/pallas_call | solution.py:313
  134.1 5.4 %collective-permute-done.24.down = bf16[3,32,1408]{2,1,0:T(8,128)(2,1)S(1)} collective-permute-done((bf16[3,32,1408]{2,1,0:T(8,128)(2,1)}, bf16[3,32,1408]{2,1,0:T(8,128)(2,1)S(1)}, u32[]{:S(2)}, u32[]{:S(2)}) %collective-permute-start.24) | collective-permute-done | bytes 270368 | tf_op jit(solution)/shard_map/ppermute | solution.py:415
  141.5 3.5 %ring_middle.6 = (bf16[3,64,1408]{2,1,0:T(8,128)(2,1)}, bf16[3,64,1408]{2,1,0:T(8,128)(2,1)}) custom-call(bf16[3,512,1408]{2,1,0:T(8,128)(2,1)} %weight_grads.5.own.own_a.own_b, bf16[3,512,1408]{2,1,0:T(8,128)(2,1)} %collective-permute-done.22.theirs.theirs_a.theirs_b, bf16[3,512,1408]{2,1,0:T(8,128)(2,1)} %weight_grads.5.own.own_a.own_b, ...), custom_call_target="tpu_custom_call" | custom-call | tf_op jit(solution)/shard_map/ring_middle/pallas_call | solution.py:344
  148.0 5.7 %collective-permute-done.23 = bf16[128,1024]{1,0:T(8,128)(2,1)S(1)} collective-permute-done((bf16[128,1024]{1,0:T(8,128)(2,1)S(1)}, bf16[128,1024]{1,0:T(8,128)(2,1)S(1)}, u32[]{:S(2)}, u32[]{:S(2)}) %collective-permute-start.23) | collective-permute-done | bytes 262176 | tf_op jit(solution)/shard_map/ppermute | solution.py:483
  154.5 11.6 %attend_back.1 = (bf16[3,256,512]{2,1,0:T(8,128)(2,1)}, f32[128,1024]{1,0:T(8,128)}, bf16[128,1024]{1,0:T(8,128)(2,1)}) custom-call(bf16[256,1024]{1,0:T(8,128)(2,1)} %pad_maximum_fusion.3.grad.second, bf16[3,256,512]{2,1,0:T(8,128)(2,1)} %get-tuple-element.101.qkv, bf16[4,512,512]{2,1,0:T(8,128)(2,1)} %copy-done.1, ...), custom_call_target="tpu_custom_call" | custom-call | tf_op jit(solution)/shard_map/attend_back/pallas_call | solution.py:249
  167.8 3.7 %ring_middle.7 = (bf16[3,64,1408]{2,1,0:T(8,128)(2,1)}, bf16[3,64,1408]{2,1,0:T(8,128)(2,1)}) custom-call(bf16[3,512,1408]{2,1,0:T(8,128)(2,1)} %weight_grads.5.own.own_a.own_b, bf16[3,512,1408]{2,1,0:T(8,128)(2,1)} %collective-permute-done.22.theirs.theirs_a.theirs_b, bf16[3,512,1408]{2,1,0:T(8,128)(2,1)} %weight_grads.5.own.own_a.own_b, ...), custom_call_target="tpu_custom_call" | custom-call | tf_op jit(solution)/shard_map/ring_middle/pallas_call | solution.py:344
  171.5 4.2 %weight_grads.6 = bf16[4,512,512]{2,1,0:T(8,128)(2,1)} custom-call(bf16[256,1024]{1,0:T(8,128)(2,1)} %get-tuple-element.112.first, bf16[256,1024]{1,0:T(8,128)(2,1)} %pad_maximum_fusion.3.grad.second, bf16[3,256,512]{2,1,0:T(8,128)(2,1)} %get-tuple-element.110.three, bf16[256,512]{1,0:T(8,128)(2,1)} %get-tuple-element.111.last), custom_call_target="tpu_custom_call" | custom-call | tf_op jit(solution)/shard_map/weight_grads/pallas_call | solution.py:287
  178.6 4.2 %weight_grads.7.own.own_a.own_b = bf16[4,512,512]{2,1,0:T(8,128)(2,1)} custom-call(bf16[256,1024]{1,0:T(8,128)(2,1)} %get-tuple-element.112.first, bf16[256,1024]{1,0:T(8,128)(2,1)} %pad_maximum_fusion.3.grad.second, bf16[3,256,512]{2,1,0:T(8,128)(2,1)} %get-tuple-element.110.three, bf16[256,512]{1,0:T(8,128)(2,1)} %get-tuple-element.111.last), custom_call_target="tpu_custom_call" | custom-call | tf_op jit(solution)/shard_map/weight_grads/pallas_call | solution.py:287
  184.1 3.0 %ring_first.3 = (bf16[4,32,512]{2,1,0:T(8,128)(2,1)}, bf16[4,32,512]{2,1,0:T(8,128)(2,1)}) custom-call(bf16[4,512,512]{2,1,0:T(8,128)(2,1)} %weight_grads.7.own.own_a.own_b, bf16[4,512,512]{2,1,0:T(8,128)(2,1)} %copy-done), custom_call_target="tpu_custom_call" | custom-call | tf_op jit(solution)/shard_map/ring_first/pallas_call | solution.py:313
  192.5 3.7 %ring_middle.9 = (bf16[3,64,1408]{2,1,0:T(8,128)(2,1)}, bf16[3,64,1408]{2,1,0:T(8,128)(2,1)}) custom-call(bf16[3,512,1408]{2,1,0:T(8,128)(2,1)} %weight_grads.5.own.own_a.own_b, bf16[3,512,1408]{2,1,0:T(8,128)(2,1)} %collective-permute-done.22.theirs.theirs_a.theirs_b, bf16[3,512,1408]{2,1,0:T(8,128)(2,1)} %weight_grads.5.own.own_a.own_b, ...), custom_call_target="tpu_custom_call" | custom-call | tf_op jit(solution)/shard_map/ring_middle/pallas_call | solution.py:344
  199.6 3.3 %ring_middle.8 = (bf16[4,64,512]{2,1,0:T(8,128)(2,1)}, bf16[4,64,512]{2,1,0:T(8,128)(2,1)}) custom-call(bf16[4,512,512]{2,1,0:T(8,128)(2,1)} %weight_grads.7.own.own_a.own_b, bf16[4,512,512]{2,1,0:T(8,128)(2,1)} %copy-done, bf16[4,512,512]{2,1,0:T(8,128)(2,1)} %weight_grads.7.own.own_a.own_b, bf16[4,512,512]{2,1,0:T(8,128)(2,1)} %copy-done, ...), custom_call_target="tpu_custom_call" | custom-call | tf_op jit(solution)/shard_map/ring_middle/pallas_call | solution.py:344
  209.4 5.6 %collective-permute-done.35.down = bf16[4,64,512]{2,1,0:T(8,128)(2,1)S(1)} collective-permute-done((bf16[4,64,512]{2,1,0:T(8,128)(2,1)}, bf16[4,64,512]{2,1,0:T(8,128)(2,1)S(1)}, u32[]{:S(2)}, u32[]{:S(2)}) %collective-permute-start.35) | collective-permute-done | bytes 262176 | tf_op jit(solution)/shard_map/ppermute | solution.py:415
  216.1 3.3 %ring_middle.10 = (bf16[4,64,512]{2,1,0:T(8,128)(2,1)}, bf16[4,64,512]{2,1,0:T(8,128)(2,1)}) custom-call(bf16[4,512,512]{2,1,0:T(8,128)(2,1)} %weight_grads.7.own.own_a.own_b, bf16[4,512,512]{2,1,0:T(8,128)(2,1)} %copy-done, bf16[4,512,512]{2,1,0:T(8,128)(2,1)} %weight_grads.7.own.own_a.own_b, bf16[4,512,512]{2,1,0:T(8,128)(2,1)} %copy-done, ...), custom_call_target="tpu_custom_call" | custom-call | tf_op jit(solution)/shard_map/ring_middle/pallas_call | solution.py:344
  222.2 3.5 %ring_last.2 = f32[3,64,1408]{2,1,0:T(8,128)} custom-call(bf16[3,512,1408]{2,1,0:T(8,128)(2,1)} %weight_grads.5.own.own_a.own_b, bf16[3,512,1408]{2,1,0:T(8,128)(2,1)} %collective-permute-done.22.theirs.theirs_a.theirs_b, bf16[3,64,1408]{2,1,0:T(8,128)(2,1)} %copy-done.8, bf16[3,64,1408]{2,1,0:T(8,128)(2,1)} %collective-permute-done.40.up), custom_call_target="tpu_custom_call" | custom-call | tf_op jit(solution)/shard_map/ring_last/pallas_call | solution.py:363
  231.6 3.4 %ring_middle.11 = (bf16[4,64,512]{2,1,0:T(8,128)(2,1)}, bf16[4,64,512]{2,1,0:T(8,128)(2,1)}) custom-call(bf16[4,512,512]{2,1,0:T(8,128)(2,1)} %weight_grads.7.own.own_a.own_b, bf16[4,512,512]{2,1,0:T(8,128)(2,1)} %copy-done, bf16[4,512,512]{2,1,0:T(8,128)(2,1)} %weight_grads.7.own.own_a.own_b, bf16[4,512,512]{2,1,0:T(8,128)(2,1)} %copy-done, ...), custom_call_target="tpu_custom_call" | custom-call | tf_op jit(solution)/shard_map/ring_middle/pallas_call | solution.py:344
  237.0 2.7 %fusion.7 = bf16[128,1024]{1,0:T(8,128)(2,1)} fusion(s32[1024]{0:T(1024)S(1)} %fusion.59, bf16[128,1024]{1,0:T(8,128)(2,1)} %collective-permute-done.27, f32[128,1024]{1,0:T(8,128)S(1)} %get-tuple-element.171, f32[128,1024]{1,0:T(8,128)S(1)} %copy-done.23), kind=kOutput, calls=%fused_computation.8 | convolution fusion | flops 270139392 | bytes 1576960 | tf_op jit(solution)/shard_map/te,de->td/dot_general | solution.py:48
  243.5 3.3 %ring_last.3 = f32[4,64,512]{2,1,0:T(8,128)} custom-call(bf16[4,512,512]{2,1,0:T(8,128)(2,1)} %weight_grads.7.own.own_a.own_b, bf16[4,512,512]{2,1,0:T(8,128)(2,1)} %copy-done, bf16[4,64,512]{2,1,0:T(8,128)(2,1)} %copy-done.17, bf16[4,64,512]{2,1,0:T(8,128)(2,1)} %copy-done.18), custom_call_target="tpu_custom_call" | custom-call | tf_op jit(solution)/shard_map/ring_last/pallas_call | solution.py:363
  (197 shorter events, 100.1 us)
Async XLA Ops:
  3.2 10.3 %collective-permute-start.1 = (bf16[4,64,512]{2,1,0:T(8,128)(2,1)S(1)}, bf16[4,64,512]{2,1,0:T(8,128)(2,1)S(1)}, u32[]{:S(2)}, u32[]{:S(2)}) collective-permute-start(bf16[4,64,512]{2,1,0:T(8,128)(2,1)S(1)} %get-tuple-element.183), channel_id=1, source_target_pairs={{0,8},{2,10},{8,16},{10,18},{16,24},{18,26},{24,28},{26,30},{28,20... | collective-permute-start | bytes 786440 | tf_op jit(solution)/shard_map/ppermute | solution.py:412
  6.3 7.9 %collective-permute-start.2 = (bf16[4,64,512]{2,1,0:T(8,128)(2,1)S(1)}, bf16[4,64,512]{2,1,0:T(8,128)(2,1)}, u32[]{:S(2)}, u32[]{:S(2)}) collective-permute-start(bf16[4,64,512]{2,1,0:T(8,128)(2,1)S(1)} %get-tuple-element.183), channel_id=1, source_target_pairs={{0,4},{2,6},{8,0},{10,2},{16,8},{18,10},{24,16},{26,18},{28,24},{3... | collective-permute-start | bytes 786440 | tf_op jit(solution)/shard_map/ppermute | solution.py:415
  8.4 16.2 %collective-permute-start = (bf16[256,1024]{1,0:T(8,128)(2,1)S(1)}, bf16[256,1024]{1,0:T(8,128)(2,1)}, u32[]{:S(2)}, u32[]{:S(2)}) collective-permute-start(bf16[256,1024]{1,0:T(8,128)(2,1)S(1)} %fusion.6), channel_id=1, source_target_pairs={{0,1},{1,0},{2,3},{3,2},{4,5},{5,4},{6,7},{7,6},{8,9},{9,8},{10,11... | collective-permute-start | bytes 1572872 | tf_op jit(solution)/shard_map/ppermute | solution.py:483
  37.1 24.0 %collective-permute-start.9 = (bf16[4,512,512]{2,1,0:T(8,128)(2,1)S(1)}, bf16[4,512,512]{2,1,0:T(8,128)(2,1)}, u32[]{:S(2)}, u32[]{:S(2)}) collective-permute-start(bf16[4,512,512]{2,1,0:T(8,128)(2,1)S(1)} %constant_dynamic-update-slice_fusion.own_hbm), channel_id=1, source_target_pairs={{0,2},{2,0},{4,6},{6,4},{8,10},{10,8},{12,14},{14,12},{16,18},{18,... | collective-permute-start | bytes 6291464 | tf_op jit(solution)/shard_map/ppermute | solution.py:418
  37.4 14.8 %collective-permute-start.12 = (bf16[3,64,1408]{2,1,0:T(8,128)(2,1)S(1)}, bf16[3,64,1408]{2,1,0:T(8,128)(2,1)}, u32[]{:S(2)}, u32[]{:S(2)}) collective-permute-start(bf16[3,64,1408]{2,1,0:T(8,128)(2,1)S(1)} %fusion.21), channel_id=1, source_target_pairs={{0,8},{2,10},{8,16},{10,18},{16,24},{18,26},{24,28},{26,30},{28,20... | collective-permute-start | bytes 1622024 | tf_op jit(solution)/shard_map/ppermute | solution.py:412
  39.3 14.4 %collective-permute-start.13 = (bf16[3,64,1408]{2,1,0:T(8,128)(2,1)S(1)}, bf16[3,64,1408]{2,1,0:T(8,128)(2,1)S(1)}, u32[]{:S(2)}, u32[]{:S(2)}) collective-permute-start(bf16[3,64,1408]{2,1,0:T(8,128)(2,1)S(1)} %fusion.21), channel_id=1, source_target_pairs={{0,4},{2,6},{8,0},{10,2},{16,8},{18,10},{24,16},{26,18},{28,24},{3... | collective-permute-start | bytes 1622024 | tf_op jit(solution)/shard_map/ppermute | solution.py:415
  54.4 15.7 %collective-permute-start.14 = (bf16[3,64,1408]{2,1,0:T(8,128)(2,1)}, bf16[3,64,1408]{2,1,0:T(8,128)(2,1)}, u32[]{:S(2)}, u32[]{:S(2)}) collective-permute-start(bf16[3,64,1408]{2,1,0:T(8,128)(2,1)} %collective-permute-done.12), channel_id=1, source_target_pairs={{0,8},{2,10},{8,16},{10,18},{16,24},{18,26},{24,28},{26,30},{28,20... | collective-permute-start | bytes 1622024 | tf_op jit(solution)/shard_map/ppermute | solution.py:412
  55.8 16.2 %collective-permute-start.15 = (bf16[3,64,1408]{2,1,0:T(8,128)(2,1)}, bf16[3,64,1408]{2,1,0:T(8,128)(2,1)}, u32[]{:S(2)}, u32[]{:S(2)}) collective-permute-start(bf16[3,64,1408]{2,1,0:T(8,128)(2,1)} %copy-done.7), channel_id=1, source_target_pairs={{0,4},{2,6},{8,0},{10,2},{16,8},{18,10},{24,16},{26,18},{28,24},{3... | collective-permute-start | bytes 1622024 | tf_op jit(solution)/shard_map/ppermute | solution.py:415
  69.0 7.3 %collective-permute-start.10 = (bf16[128,1024]{1,0:T(8,128)(2,1)}, bf16[128,1024]{1,0:T(8,128)(2,1)S(1)}, u32[]{:S(2)}, u32[]{:S(2)}) collective-permute-start(bf16[128,1024]{1,0:T(8,128)(2,1)} %get-tuple-element.79), channel_id=1, source_target_pairs={{0,1},{1,0},{2,3},{3,2},{4,5},{5,4},{6,7},{7,6},{8,9},{9,8},{10,11... | collective-permute-start | bytes 786440 | tf_op jit(solution)/shard_map/ppermute | solution.py:483
  73.9 13.0 %collective-permute-start.16 = (bf16[3,64,1408]{2,1,0:T(8,128)(2,1)}, bf16[3,64,1408]{2,1,0:T(8,128)(2,1)S(1)}, u32[]{:S(2)}, u32[]{:S(2)}) collective-permute-start(bf16[3,64,1408]{2,1,0:T(8,128)(2,1)} %collective-permute-done.14), channel_id=1, source_target_pairs={{0,8},{2,10},{8,16},{10,18},{16,24},{18,26},{24,28},{26,30},{28,20... | collective-permute-start | bytes 1622024 | tf_op jit(solution)/shard_map/ppermute | solution.py:412
  74.4 12.9 %collective-permute-start.17 = (bf16[3,64,1408]{2,1,0:T(8,128)(2,1)}, bf16[3,64,1408]{2,1,0:T(8,128)(2,1)S(1)}, u32[]{:S(2)}, u32[]{:S(2)}) collective-permute-start(bf16[3,64,1408]{2,1,0:T(8,128)(2,1)} %collective-permute-done.15), channel_id=1, source_target_pairs={{0,4},{2,6},{8,0},{10,2},{16,8},{18,10},{24,16},{26,18},{28,24},{3... | collective-permute-start | bytes 1622024 | tf_op jit(solution)/shard_map/ppermute | solution.py:415
  95.3 9.6 %collective-permute-start.20 = (bf16[3,512,1408]{2,1,0:T(8,128)(2,1)}, bf16[3,512,1408]{2,1,0:T(8,128)(2,1)}, u32[]{:S(2)}, u32[]{:S(2)}) collective-permute-start(bf16[3,512,1408]{2,1,0:T(8,128)(2,1)} %constant_dynamic-update-slice_fusion.9.own_hbm), channel_id=1, source_target_pairs={{0,2},{2,0},{4,6},{6,4},{8,10},{10,8},{12,14},{14,12},{16,18},{18,... | collective-permute-start | bytes 12976136 | tf_op jit(solution)/shard_map/ppermute | solution.py:418
  95.3 8.7 %collective-permute-start.11 = (bf16[128,1024]{1,0:T(8,128)(2,1)S(1)}, bf16[128,1024]{1,0:T(8,128)(2,1)S(1)}, u32[]{:S(2)}, u32[]{:S(2)}) collective-permute-start(bf16[128,1024]{1,0:T(8,128)(2,1)S(1)} %fusion.33), channel_id=1, source_target_pairs={{0,1},{1,0},{2,3},{3,2},{4,5},{5,4},{6,7},{7,6},{8,9},{9,8},{10,11... | collective-permute-start | bytes 786440 | tf_op jit(solution)/shard_map/ppermute | solution.py:483
  120.2 7.7 %collective-permute-start.22 = (bf16[3,512,1408]{2,1,0:T(8,128)(2,1)}, bf16[3,512,1408]{2,1,0:T(8,128)(2,1)}, u32[]{:S(2)}, u32[]{:S(2)}) collective-permute-start(bf16[3,512,1408]{2,1,0:T(8,128)(2,1)} %weight_grads.4), channel_id=1, source_target_pairs={{0,2},{2,0},{4,6},{6,4},{8,10},{10,8},{12,14},{14,12},{16,18},{18,... | collective-permute-start | bytes 12976136 | tf_op jit(solution)/shard_map/ppermute | solution.py:418
  120.2 12.6 %collective-permute-start.21 = (bf16[128,1024]{1,0:T(8,128)(2,1)S(1)}, bf16[128,1024]{1,0:T(8,128)(2,1)S(1)}, u32[]{:S(2)}, u32[]{:S(2)}) collective-permute-start(bf16[128,1024]{1,0:T(8,128)(2,1)S(1)} %copy-done.24), channel_id=1, source_target_pairs={{0,1},{1,0},{2,3},{3,2},{4,5},{5,4},{6,7},{7,6},{8,9},{9,8},{10,11... | collective-permute-start | bytes 786440 | tf_op jit(solution)/shard_map/ppermute | solution.py:483
  130.8 8.7 %collective-permute-start.24 = (bf16[3,32,1408]{2,1,0:T(8,128)(2,1)}, bf16[3,32,1408]{2,1,0:T(8,128)(2,1)S(1)}, u32[]{:S(2)}, u32[]{:S(2)}) collective-permute-start(bf16[3,32,1408]{2,1,0:T(8,128)(2,1)} %get-tuple-element.93), channel_id=1, source_target_pairs={{0,4},{2,6},{8,0},{10,2},{16,8},{18,10},{24,16},{26,18},{28,24},{3... | collective-permute-start | bytes 811016 | tf_op jit(solution)/shard_map/ppermute | solution.py:415
  132.3 8.5 %collective-permute-start.25 = (bf16[3,32,1408]{2,1,0:T(8,128)(2,1)}, bf16[3,32,1408]{2,1,0:T(8,128)(2,1)S(1)}, u32[]{:S(2)}, u32[]{:S(2)}) collective-permute-start(bf16[3,32,1408]{2,1,0:T(8,128)(2,1)} %get-tuple-element.94), channel_id=1, source_target_pairs={{0,8},{2,10},{8,16},{10,18},{16,24},{18,26},{24,28},{26,30},{28,20... | collective-permute-start | bytes 811016 | tf_op jit(solution)/shard_map/ppermute | solution.py:412
  145.0 21.1 %collective-permute-start.28 = (bf16[3,64,1408]{2,1,0:T(8,128)(2,1)}, bf16[3,64,1408]{2,1,0:T(8,128)(2,1)S(1)}, u32[]{:S(2)}, u32[]{:S(2)}) collective-permute-start(bf16[3,64,1408]{2,1,0:T(8,128)(2,1)} %get-tuple-element.98), channel_id=1, source_target_pairs={{0,4},{2,6},{8,0},{10,2},{16,8},{18,10},{24,16},{26,18},{28,24},{3... | collective-permute-start | bytes 1622024 | tf_op jit(solution)/shard_map/ppermute | solution.py:415
  146.5 19.7 %collective-permute-start.29 = (bf16[3,64,1408]{2,1,0:T(8,128)(2,1)}, bf16[3,64,1408]{2,1,0:T(8,128)(2,1)S(1)}, u32[]{:S(2)}, u32[]{:S(2)}) collective-permute-start(bf16[3,64,1408]{2,1,0:T(8,128)(2,1)} %get-tuple-element.99), channel_id=1, source_target_pairs={{0,8},{2,10},{8,16},{10,18},{16,24},{18,26},{24,28},{26,30},{28,20... | collective-permute-start | bytes 1622024 | tf_op jit(solution)/shard_map/ppermute | solution.py:412
  175.6 7.1 %collective-permute-start.30 = (bf16[4,512,512]{2,1,0:T(8,128)(2,1)}, bf16[4,512,512]{2,1,0:T(8,128)(2,1)S(1)}, u32[]{:S(2)}, u32[]{:S(2)}) collective-permute-start(bf16[4,512,512]{2,1,0:T(8,128)(2,1)} %weight_grads.6), channel_id=1, source_target_pairs={{0,2},{2,0},{4,6},{6,4},{8,10},{10,8},{12,14},{14,12},{16,18},{18,... | collective-permute-start | bytes 6291464 | tf_op jit(solution)/shard_map/ppermute | solution.py:418
  175.6 15.4 %collective-permute-start.33 = (bf16[3,64,1408]{2,1,0:T(8,128)(2,1)}, bf16[3,64,1408]{2,1,0:T(8,128)(2,1)}, u32[]{:S(2)}, u32[]{:S(2)}) collective-permute-start(bf16[3,64,1408]{2,1,0:T(8,128)(2,1)} %get-tuple-element.107), channel_id=1, source_target_pairs={{0,4},{2,6},{8,0},{10,2},{16,8},{18,10},{24,16},{26,18},{28,24},{3... | collective-permute-start | bytes 1622024 | tf_op jit(solution)/shard_map/ppermute | solution.py:415
  177.0 15.4 %collective-permute-start.34 = (bf16[3,64,1408]{2,1,0:T(8,128)(2,1)}, bf16[3,64,1408]{2,1,0:T(8,128)(2,1)}, u32[]{:S(2)}, u32[]{:S(2)}) collective-permute-start(bf16[3,64,1408]{2,1,0:T(8,128)(2,1)} %get-tuple-element.108), channel_id=1, source_target_pairs={{0,8},{2,10},{8,16},{10,18},{16,24},{18,26},{24,28},{26,30},{28,20... | collective-permute-start | bytes 1622024 | tf_op jit(solution)/shard_map/ppermute | solution.py:412
  177.6 11.5 %collective-permute-start.26 = (bf16[128,1024]{1,0:T(8,128)(2,1)}, bf16[128,1024]{1,0:T(8,128)(2,1)}, u32[]{:S(2)}, u32[]{:S(2)}) collective-permute-start(bf16[128,1024]{1,0:T(8,128)(2,1)} %get-tuple-element.102), channel_id=1, source_target_pairs={{0,1},{1,0},{2,3},{3,2},{4,5},{5,4},{6,7},{7,6},{8,9},{9,8},{10,11... | collective-permute-start | bytes 786440 | tf_op jit(solution)/shard_map/ppermute | solution.py:483
  187.1 11.1 %collective-permute-start.31 = (bf16[4,32,512]{2,1,0:T(8,128)(2,1)}, bf16[4,32,512]{2,1,0:T(8,128)(2,1)S(1)}, u32[]{:S(2)}, u32[]{:S(2)}) collective-permute-start(bf16[4,32,512]{2,1,0:T(8,128)(2,1)} %get-tuple-element.113), channel_id=1, source_target_pairs={{0,4},{2,6},{8,0},{10,2},{16,8},{18,10},{24,16},{26,18},{28,24},{3... | collective-permute-start | bytes 393224 | tf_op jit(solution)/shard_map/ppermute | solution.py:415
  188.5 9.8 %collective-permute-start.32 = (bf16[4,32,512]{2,1,0:T(8,128)(2,1)}, bf16[4,32,512]{2,1,0:T(8,128)(2,1)S(1)}, u32[]{:S(2)}, u32[]{:S(2)}) collective-permute-start(bf16[4,32,512]{2,1,0:T(8,128)(2,1)} %get-tuple-element.114), channel_id=1, source_target_pairs={{0,8},{2,10},{8,16},{10,18},{16,24},{18,26},{24,28},{26,30},{28,20... | collective-permute-start | bytes 393224 | tf_op jit(solution)/shard_map/ppermute | solution.py:412
  189.2 47.9 %collective-permute-start.27 = (bf16[128,1024]{1,0:T(8,128)(2,1)}, bf16[128,1024]{1,0:T(8,128)(2,1)}, u32[]{:S(2)}, u32[]{:S(2)}) collective-permute-start(bf16[128,1024]{1,0:T(8,128)(2,1)} %get-tuple-element.103), channel_id=1, source_target_pairs={{0,1},{1,0},{2,3},{3,2},{4,5},{5,4},{6,7},{7,6},{8,9},{9,8},{10,11... | collective-permute-start | bytes 786440 | tf_op jit(solution)/shard_map/ppermute | solution.py:483
  196.2 25.3 %collective-permute-start.39 = (bf16[3,64,1408]{2,1,0:T(8,128)(2,1)}, bf16[3,64,1408]{2,1,0:T(8,128)(2,1)S(1)}, u32[]{:S(2)}, u32[]{:S(2)}) collective-permute-start(bf16[3,64,1408]{2,1,0:T(8,128)(2,1)} %get-tuple-element.119), channel_id=1, source_target_pairs={{0,4},{2,6},{8,0},{10,2},{16,8},{18,10},{24,16},{26,18},{28,24},{3... | collective-permute-start | bytes 1622024 | tf_op jit(solution)/shard_map/ppermute | solution.py:415
  197.5 23.9 %collective-permute-start.40 = (bf16[3,64,1408]{2,1,0:T(8,128)(2,1)}, bf16[3,64,1408]{2,1,0:T(8,128)(2,1)}, u32[]{:S(2)}, u32[]{:S(2)}) collective-permute-start(bf16[3,64,1408]{2,1,0:T(8,128)(2,1)} %get-tuple-element.120), channel_id=1, source_target_pairs={{0,8},{2,10},{8,16},{10,18},{16,24},{18,26},{24,28},{26,30},{28,20... | collective-permute-start | bytes 1622024 | tf_op jit(solution)/shard_map/ppermute | solution.py:412
  202.8 12.1 %collective-permute-start.35 = (bf16[4,64,512]{2,1,0:T(8,128)(2,1)}, bf16[4,64,512]{2,1,0:T(8,128)(2,1)S(1)}, u32[]{:S(2)}, u32[]{:S(2)}) collective-permute-start(bf16[4,64,512]{2,1,0:T(8,128)(2,1)} %get-tuple-element.121), channel_id=1, source_target_pairs={{0,4},{2,6},{8,0},{10,2},{16,8},{18,10},{24,16},{26,18},{28,24},{3... | collective-permute-start | bytes 786440 | tf_op jit(solution)/shard_map/ppermute | solution.py:415
  204.1 11.9 %collective-permute-start.36 = (bf16[4,64,512]{2,1,0:T(8,128)(2,1)}, bf16[4,64,512]{2,1,0:T(8,128)(2,1)}, u32[]{:S(2)}, u32[]{:S(2)}) collective-permute-start(bf16[4,64,512]{2,1,0:T(8,128)(2,1)} %get-tuple-element.122), channel_id=1, source_target_pairs={{0,8},{2,10},{8,16},{10,18},{16,24},{18,26},{24,28},{26,30},{28,20... | collective-permute-start | bytes 786440 | tf_op jit(solution)/shard_map/ppermute | solution.py:412
  219.4 10.8 %collective-permute-start.37 = (bf16[4,64,512]{2,1,0:T(8,128)(2,1)}, bf16[4,64,512]{2,1,0:T(8,128)(2,1)S(1)}, u32[]{:S(2)}, u32[]{:S(2)}) collective-permute-start(bf16[4,64,512]{2,1,0:T(8,128)(2,1)} %get-tuple-element.127), channel_id=1, source_target_pairs={{0,4},{2,6},{8,0},{10,2},{16,8},{18,10},{24,16},{26,18},{28,24},{3... | collective-permute-start | bytes 786440 | tf_op jit(solution)/shard_map/ppermute | solution.py:415
  220.6 9.7 %collective-permute-start.38 = (bf16[4,64,512]{2,1,0:T(8,128)(2,1)}, bf16[4,64,512]{2,1,0:T(8,128)(2,1)S(1)}, u32[]{:S(2)}, u32[]{:S(2)}) collective-permute-start(bf16[4,64,512]{2,1,0:T(8,128)(2,1)} %get-tuple-element.128), channel_id=1, source_target_pairs={{0,8},{2,10},{8,16},{10,18},{16,24},{18,26},{24,28},{26,30},{28,20... | collective-permute-start | bytes 786440 | tf_op jit(solution)/shard_map/ppermute | solution.py:412
  (39 other events, 244.8 us)
where the time goes:
time: 255 us; the launch traced here: 253 us
  Pallas kernels  81.7 us (32%)
  waiting for transfers between devices  75.4 us (30%)
  starting transfers between devices  42.9 us (17%)
  local copies, waits for them, and re-layouts  28.7 us (11%)
  other arithmetic  17.4 us (7%)
  matrix products  5.8 us (2%)
    ppermute x16, waiting for transfers between devices, ahead(): return lax.ppermute(block, 'dp', self.forward)  38.1 us
    unnamed x70, local copies, waits for them, and re-layouts  22.1 us
    pallas_call x6, Pallas kernels, middle_call(): pl.pallas_call(middle_kernel, grid=(planes,), out_shape=(shape((planes, r...  20.9 us
    ppermute x16, waiting for transfers between devices, back(): return lax.ppermute(block, 'dp', self.backward)  20.6 us
    pallas_call x4, Pallas kernels, weight_grads(): pl.pallas_call(outer_kernel, grid=(planes,), out_shape=shape((planes, cut...  18.3 us
    ppermute x16, starting transfers between devices, back(): return lax.ppermute(block, 'dp', self.backward)  17.2 us
    ppermute x16, starting transfers between devices, ahead(): return lax.ppermute(block, 'dp', self.forward)  16.7 us
    ppermute x8, waiting for transfers between devices, swap(): return lax.ppermute(block, 'tensor', [(0, 1), (1, 0)])  15.1 us
  transfers between devices with their start and end apart: 44, of which 25 were waited for; matrix products, arithmetic and copies ran while one was open for 15% of the time, Pallas kernels for 20%

commit v1 on v0

--- a/solution.py
+++ b/solution.py
@@ -64,38 +64,73 @@
     return jax.ShapeDtypeStruct(dims, kind)
 
 
-ANYWHERE = pl.BlockSpec(memory_space=pl.ANY)
+ANYWHERE = pl.BlockSpec(memory_space=pltpu.HBM)
+LONG = pl.CostEstimate(flops=10**11, bytes_accessed=10**9, transcendentals=0)
+NEAR = 2**20
+SHORT = pl.CostEstimate(flops=1000, bytes_accessed=1000, transcendentals=0)
 WHOLE = pl.BlockSpec(memory_space=pltpu.VMEM)
 
 
-def load_planes(own_hbm, oth_hbm, own, oth, sems):
+def load_planes(parts, own, oth, sems):
+    half = len(parts) // 2
     copies = []
     for plane in range(own.shape[0]):
-        pair = (
-            pltpu.make_async_copy(own_hbm.at[plane], own.at[plane], sems.at[0, plane]),
-            pltpu.make_async_copy(oth_hbm.at[plane], oth.at[plane], sems.at[1, plane]),
-        )
-        copies.append(pair)
+        copies.append([])
+        for k, part in enumerate(parts):
+            at = sum(q.shape[1] for q in parts[k // half * half : k])
+            target = (own if k < half else oth).at[plane, pl.ds(at, part.shape[1])]
+            copies[plane].append(pltpu.make_async_copy(part.at[plane], target, sems.at[k, plane]))
     return copies
 
 
 def begin(copies, order):
     for plane in order:
-        copies[plane][0].start()
-        copies[plane][1].start()
+        for copy in copies[plane]:
+            copy.start()
 
 
 def finish(copies, plane):
-    copies[plane][0].wait()
-    copies[plane][1].wait()
-
-
-def planes_scratch(block):
+    for copy in copies[plane]:
+        copy.wait()
+
+
+def held_block(own):
+    return (own[0].shape[0], sum(part.shape[1] for part in own), own[0].shape[2])
+
+
+def planes_scratch(own):
+    block = held_block(own)
     return [
         pltpu.VMEM(block, BF),
         pltpu.VMEM(block, BF),
-        pltpu.SemaphoreType.DMA((2, block[0])),
+        pltpu.SemaphoreType.DMA((2 * len(own), block[0])),
     ]
+
+
+def stack_kernel(*refs):
+    pieces, out, sems = refs[:-2], refs[-2], refs[-1]
+    copies, at = [], 0
+    for k, piece in enumerate(pieces):
+        copies.append(
+            pltpu.make_async_copy(piece, out.at[:, pl.ds(at, piece.shape[1])], sems.at[k])
+        )
+        copies[k].start()
+        at += piece.shape[1]
+    for copy in copies:
+        copy.wait()
+
+
+def stack_call(pieces, far):
+    planes, _, lanes = pieces[0].shape
+    return pl.pallas_call(
+        stack_kernel,
+        out_shape=shape((planes, sum(p.shape[1] for p in pieces), lanes), BF),
+        in_specs=[WHOLE] * len(pieces),
+        out_specs=ANYWHERE,
+        scratch_shapes=[pltpu.SemaphoreType.DMA((len(pieces),))],
+        name="stack_rows",
+        cost_estimate=LONG,
+    )(*pieces[:far], *[close(piece) for piece in pieces[far:]])
 
 
 def swing(values, cosine, sine):
@@ -117,8 +152,9 @@
     return raised * (1.0 / jnp.sum(raised, axis=-1, keepdims=True))
 
 
-def attend_kernel(x, own_hbm, oth_hbm, docs, docs_row, cos, sin, qkv, mixed, hat, part, away, own, oth, sems):
-    copies = load_planes(own_hbm, oth_hbm, own, oth, sems)
+def attend_kernel(x, docs, docs_row, cos, sin, *refs):
+    parts, (qkv, mixed, hat, part, away, own, oth, sems) = refs[:-8], refs[-8:]
+    copies = load_planes(parts, own, oth, sems)
     begin(copies, range(4))
     normed, _ = normalize(x[...].astype(F32))
     hat[...] = normed.astype(BF)
@@ -144,7 +180,7 @@
 
 def attend_call(x, own, oth, docs, cos, sin):
     group, width = x.shape
-    planes, cut, lanes = own.shape
+    lanes = own[0].shape[2]
     return pl.pallas_call(
         attend_kernel,
         out_shape=(
@@ -154,15 +190,18 @@
             shape((group // 2, width), F32),
             shape((group // 2, width), BF),
         ),
-        in_specs=[WHOLE, ANYWHERE, ANYWHERE, WHOLE, WHOLE, WHOLE, WHOLE],
+        in_specs=[WHOLE] * 5 + [ANYWHERE] * (2 * len(own)),
         out_specs=(WHOLE,) * 5,
-        scratch_shapes=planes_scratch(own.shape),
+        scratch_shapes=planes_scratch(own),
         name="attend",
-    )(x, own, oth, docs[:, None], docs[None, :], cos, sin)
-
-
-def mlp_kernel(hat, cot, own_hbm, oth_hbm, three, part, away, out_part, out_away, own, oth, sems, gate, upper, back):
-    copies = load_planes(own_hbm, oth_hbm, own, oth, sems)
+        cost_estimate=SHORT,
+    )(x, docs[:, None], docs[None, :], cos, sin, *own, *oth)
+
+
+def mlp_kernel(hat, cot, *refs):
+    parts, refs = refs[:-11], refs[-11:]
+    three, part, away, out_part, out_away, own, oth, sems, gate, upper, back = refs
+    copies = load_planes(parts, own, oth, sems)
     begin(copies, range(3))
     cut = own.shape[1]
     count = part.shape[0]
@@ -197,7 +236,7 @@
 
 def mlp_call(hat, cot, own, oth):
     group, width = hat.shape
-    hidden = own.shape[2]
+    hidden = own[0].shape[2]
     half = group // 2
     return pl.pallas_call(
         mlp_kernel,
@@ -208,15 +247,17 @@
             shape((half, width), F32),
             shape((half, width), BF),
         ),
-        in_specs=[WHOLE, WHOLE, ANYWHERE, ANYWHERE],
+        in_specs=[WHOLE] * 2 + [ANYWHERE] * (2 * len(own)),
         out_specs=(WHOLE,) * 5,
-        scratch_shapes=planes_scratch(own.shape) + [pltpu.VMEM((group, hidden), F32)] * 3,
+        scratch_shapes=planes_scratch(own) + [pltpu.VMEM((group, hidden), F32)] * 3,
         name="mlp",
-    )(hat, cot, own, oth)
-
-
-def back_kernel(grad, qkv, own_hbm, oth_hbm, docs, docs_row, cos, sin, three, part, away, own, oth, sems, gmix, wide):
-    copies = load_planes(own_hbm, oth_hbm, own, oth, sems)
+        cost_estimate=SHORT,
+    )(hat, cot, *own, *oth)
+
+
+def back_kernel(grad, qkv, docs, docs_row, cos, sin, *refs):
+    parts, (three, part, away, own, oth, sems, gmix, wide) = refs[:-8], refs[-8:]
+    copies = load_planes(parts, own, oth, sems)
     begin(copies, (3, 0, 1, 2))
     cut = own.shape[1]
     count = part.shape[0]
@@ -245,7 +286,7 @@
 
 def back_call(grad, qkv, own, oth, docs, cos, sin):
     group, width = grad.shape
-    lanes = own.shape[2]
+    lanes = own[0].shape[2]
     return pl.pallas_call(
         back_kernel,
         out_shape=(
@@ -253,25 +294,34 @@
             shape((group // 2, width), F32),
             shape((group // 2, width), BF),
         ),
-        in_specs=[WHOLE, WHOLE, ANYWHERE, ANYWHERE, WHOLE, WHOLE, WHOLE, WHOLE],
+        in_specs=[WHOLE] * 6 + [ANYWHERE] * (2 * len(own)),
         out_specs=(WHOLE,) * 3,
-        scratch_shapes=planes_scratch(own.shape)
+        scratch_shapes=planes_scratch(own)
         + [pltpu.VMEM((group, lanes), BF), pltpu.VMEM((2, group, lanes), F32)],
         name="attend_back",
-    )(grad, qkv, own, oth, docs[:, None], docs[None, :], cos, sin)
-
-
-def outer_kernel(first, second, three, last, out):
+        cost_estimate=SHORT,
+    )(grad, qkv, docs[:, None], docs[None, :], cos, sin, *own, *oth)
+
+
+def outer_kernel(first, second, three, last, out, turned):
     plane = pl.program_id(0)
     split = pl.num_programs(0) - 1
 
+    @pl.when(plane == 0)
+    def _():
+        turned[...] = first[...].T
+
+    @pl.when(plane == split)
+    def _():
+        turned[...] = second[...].T
+
     @pl.when(plane < split)
     def _():
-        out[0] = tn(first[...], three[0]).astype(BF)
+        out[0] = nn(turned[...], three[0]).astype(BF)
 
     @pl.when(plane == split)
     def _():
-        out[0] = tn(second[...], last[...]).astype(BF)
+        out[0] = nn(turned[...], last[...]).astype(BF)
 
 
 def weight_grads(first, second, three, last, side):
@@ -295,79 +345,90 @@
             last_spec,
         ],
         out_specs=pl.BlockSpec((1, cut, lanes), lambda i: (i, 0, 0)),
+        scratch_shapes=[pltpu.VMEM((cut, group), BF)],
         name="weight_grads",
+        cost_estimate=LONG,
     )(first, second, three, last)
 
 
-def first_kernel(own, theirs, down, up):
-    total = (own[...].astype(F32) + theirs[...].astype(F32)).astype(BF)
-    h = total.shape[1] // 2
-    down[...] = total[:, :h]
-    up[...] = total[:, h:]
+def ring_sum(name, own, theirs, got, j, count, outs, compute):
+    planes, _, lanes = own.shape
+    near = theirs.size <= NEAR
+    n_got, n_out = len(got), len(outs)
+    n_far = 1 if near else 2
+
+    def kernel(*refs):
+        sources = refs[:2]
+        received = refs[2 : 2 + n_got]
+        made = refs[2 + n_got : 2 + n_got + n_out]
+        held = refs[2 + n_got + n_out : -1]
+        sems = refs[-1]
+        copies = []
+        for plane in range(planes):
+            copies.append(
+                [
+                    pltpu.make_async_copy(
+                        sources[k].at[plane, pl.ds(j, count)], held[k].at[plane], sems.at[k, plane]
+                    )
+                    for k in range(n_far)
+                ]
+            )
+            for copy in copies[plane]:
+                copy.start()
+        for plane in range(planes):
+            for copy in copies[plane]:
+                copy.wait()
+            second = sources[1][plane, j : j + count] if near else held[1][plane]
+            total = held[0][plane].astype(F32) + second.astype(F32)
+            compute(total, [r[plane].astype(F32) for r in received], [m.at[plane] for m in made])
+
+    return pl.pallas_call(
+        kernel,
+        out_shape=tuple(shape((planes, r, lanes), kind) for r, kind in outs),
+        in_specs=[ANYWHERE, WHOLE if near else ANYWHERE] + [WHOLE] * n_got,
+        out_specs=(WHOLE,) * n_out,
+        scratch_shapes=[pltpu.VMEM((planes, count, lanes), BF)] * n_far
+        + [pltpu.SemaphoreType.DMA((n_far, planes))],
+        name=name,
+        cost_estimate=SHORT,
+    )(own, theirs, *got)
 
 
 def first_call(own, theirs, rows, j):
-    planes, _, lanes = own.shape
-    block = pl.BlockSpec((1, rows, lanes), lambda i: (i, j, 0))
-    out = pl.BlockSpec((1, rows // 2, lanes), lambda i: (i, 0, 0))
-    return pl.pallas_call(
-        first_kernel,
-        grid=(planes,),
-        out_shape=(shape((planes, rows // 2, lanes), BF),) * 2,
-        in_specs=[block, block],
-        out_specs=(out, out),
-        name="ring_first",
-    )(own, theirs)
-
-
-def middle_kernel(own_a, theirs_a, own_b, theirs_b, down, up, out_a, out_b):
-    a = own_a[...].astype(F32) + theirs_a[...].astype(F32)
-    b = own_b[...].astype(F32) + theirs_b[...].astype(F32)
-    rows = a.shape[1]
+    h = rows // 2
+
+    def compute(total, got, made):
+        made[0][...] = total[:h].astype(BF)
+        made[1][...] = total[h:].astype(BF)
+
+    return ring_sum("ring_first", own, theirs, (), j * rows, rows, ((h, BF), (h, BF)), compute)
+
+
+def middle_call(own, theirs, down, up, rows, j):
     h = down.shape[1]
-    if h == rows:
-        out_a[...] = (a + down[...].astype(F32)).astype(BF)
-        out_b[...] = (b + up[...].astype(F32)).astype(BF)
-    else:
-        out_a[:, :h] = (a[:, :h] + down[...].astype(F32)).astype(BF)
-        out_a[:, h:] = a[:, h:].astype(BF)
-        out_b[:, :h] = b[:, :h].astype(BF)
-        out_b[:, h:] = (b[:, h:] + up[...].astype(F32)).astype(BF)
-
-
-def middle_call(own, theirs, down, up, rows, j):
-    planes, _, lanes = own.shape
-    left = pl.BlockSpec((1, rows, lanes), lambda i: (i, j, 0))
-    right = pl.BlockSpec((1, rows, lanes), lambda i: (i, j + 1, 0))
-    got = pl.BlockSpec((1, down.shape[1], lanes), lambda i: (i, 0, 0))
-    out = pl.BlockSpec((1, rows, lanes), lambda i: (i, 0, 0))
-    return pl.pallas_call(
-        middle_kernel,
-        grid=(planes,),
-        out_shape=(shape((planes, rows, lanes), BF),) * 2,
-        in_specs=[left, left, right, right, got, got],
-        out_specs=(out, out),
-        name="ring_middle",
-    )(own, theirs, own, theirs, down, up)
-
-
-def last_kernel(own, theirs, down, up, out):
-    out[...] = (own[...].astype(F32) + theirs[...].astype(F32)) + (
-        down[...].astype(F32) + up[...].astype(F32)
+
+    def compute(total, got, made):
+        a, b = total[:rows], total[rows:]
+        made[0][:h] = (a[:h] + got[0]).astype(BF)
+        made[1][rows - h :] = (b[rows - h :] + got[1]).astype(BF)
+        if h < rows:
+            made[0][h:] = a[h:].astype(BF)
+            made[1][: rows - h] = b[: rows - h].astype(BF)
+
+    return ring_sum(
+        "ring_middle", own, theirs, (down, up), j * rows, 2 * rows, ((rows, BF), (rows, BF)), compute
     )
 
 
 def last_call(own, theirs, down, up, rows):
-    planes, _, lanes = own.shape
-    block = pl.BlockSpec((1, rows, lanes), lambda i: (i, 0, 0))
-    return pl.pallas_call(
-        last_kernel,
-        grid=(planes,),
-        out_shape=shape((planes, rows, lanes), F32),
-        in_specs=[block] * 4,
-        out_specs=block,
-        name="ring_last",
-    )(own, theirs, down, up)
+    def compute(total, got, made):
+        made[0][...] = total + (got[0] + got[1])
+
+    return ring_sum("ring_last", own, theirs, (down, up), 0, rows, ((rows, F32),), compute)[0]
+
+
+def close(value):
+    return pltpu.with_memory_space_constraint(value, pltpu.VMEM)
 
 
 def tie(value, *after):
@@ -425,6 +486,7 @@
         self.pieces = [block]
         self.a = self.b = block
         self.left = ring.chips // 2 if ring.ringed else 0
+        self.kept = ring.chips - 3
 
     def step(self, *after):
         if self.left == 0:
@@ -437,19 +499,29 @@
         self.a, self.b = self.ring.ahead(a), self.ring.back(b)
         self.pieces += [self.a, self.b]
 
+    def early(self, *after):
+        if not self.ring.ringed:
+            return
+        part = stack_call([tie(self.pieces[0], *after)] + self.pieces[1 : self.kept], 1)
+        self.parts = [(part, self.ring.across(part))]
+        self.pieces = self.pieces[self.kept :]
+
     def done(self):
         if self.ring.ringed:
-            own = jnp.concatenate(self.pieces, axis=1)
+            part = stack_call(self.pieces[-4:], 0)
+            self.parts.append((part, self.ring.across(part)))
         else:
-            own = lax.all_gather(
+            part = lax.all_gather(
                 self.block, "dp", axis=1, tiled=True, axis_index_groups=self.ring.groups
             )
-        return own, self.ring.across(own)
+            self.parts = [(part, self.ring.across(part))]
+        return tuple(zip(*self.parts))
 
 
 class Reduce:
     def __init__(self, ring, own, theirs):
-        self.ring, self.own, self.theirs = ring, own, theirs
+        near = ring.ringed and theirs.size <= NEAR
+        self.ring, self.own, self.theirs = ring, own, close(theirs) if near else theirs
         self.rows = own.shape[1] // ring.chips
         self.left = ring.chips // 2 if ring.ringed else 0
         self.down = self.up = None
@@ -467,7 +539,7 @@
             down, up = tie((down, up), *after)
         self.left -= 1
         self.sent = (down, up)
-        self.down, self.up = self.ring.back(down), self.ring.ahead(up)
+        self.down, self.up = close(self.ring.back(down)), close(self.ring.ahead(up))
 
     def done(self, *after):
         if not self.ring.ringed:
@@ -520,9 +592,10 @@
     cot_all = jnp.concatenate([moved[count:], moved_other[count:]], axis=0)
 
     gather_a.step(moved)
+    gather_a.early()
     gather_a.step(cosine, sine)
-    gather_b.step(*gather_a.pieces[3:5])
-    gather_a.step(tokens_all, cot_all)
+    gather_a.step(tokens_all, cot_all, gather_b.a, gather_b.b)
+    gather_b.step(*gather_a.pieces[:2])
     own_a, oth_a = gather_a.done()
 
     normed_one, factor_one = normalize(moved[:count].astype(F32))
@@ -532,8 +605,9 @@
     residual = moved[:count].astype(F32) + part + swapped.astype(F32)
     normed_two, factor_two = normalize(residual)
     hat_own = normed_two.astype(BF)
+    gather_b.early(hat_own)
     hat_two = jnp.concatenate([hat_own, swap(hat_own)], axis=0)
-    gather_b.step(hat_own)
+    gather_b.step(hat_two)
     own_b, oth_b = gather_b.done()
 
     three_b, part, away, out_part, out_away = mlp_call(hat_two, cot_all, own_b, oth_b)
@@ -547,7 +621,7 @@
     grad_residual = moved[count:].astype(F32) + norm_back(grad_hat_two, normed_two, factor_two)
     grad_res_own = grad_residual.astype(BF)
     grad_res_all = jnp.concatenate([grad_res_own, swap(grad_res_own)], axis=0)
-    reduce_b.step(grad_res_own)
+    reduce_b.step(grad_res_all)
     three_a, part, away = back_call(
         tie(grad_res_all, *reduce_b.sent), qkv, own_a, oth_a, docs, cosine, sine
     )

time: 255 us -> 224 us (0.88)
  waiting for transfers between devices: 75.4 us -> 51.7 us
  local copies, waits for them, and re-layouts: 28.7 us -> 14.6 us
  other arithmetic: 17.4 us -> 23.4 us
    ppermute x16, waiting for transfers between devices: 38.1 us -> 16.5 us  [ahead(): return lax.ppermute(block, 'dp', self.forward)]
    unnamed x70 -> x89, local copies, waits for them, and re-layouts: 22.1 us -> 6.02 us
    ppermute x16, starting transfers between devices: 17.2 us -> 8.76 us  [back(): return lax.ppermute(block, 'dp', self.backward)]
    ppermute x16, starting transfers between devices: 16.7 us -> 25.1 us  [ahead(): return lax.ppermute(block, 'dp', self.forward)]
    ppermute x16, waiting for transfers between devices: 20.6 us -> 16.3 us  [back(): return lax.ppermute(block, 'dp', self.backward)]
    ppermute x4 -> x6, waiting for transfers between devices: 1.56 us -> 4.46 us  [across(): return lax.ppermute(block, 'dp', self.core)]
    slice x4, local copies, waits for them, and re-layouts: 0.06 us -> 2.78 us  [step(): a, b = (a[:, :rows // 2], b[:, rows // 2:])]
    pallas_call x10 -> x14, Pallas kernels: 33.6 us -> 32.7 us  [the longest x10 24.5 us: ring_sum(): pl.pallas_call(kernel, out_shape=tuple((shape((planes, r, lanes), kind) f...]
  transfers between devices with their start and end apart: 44 -> 46, of which waited for: 25 -> 23; matrix products, arithmetic and copies ran while one was open for 15% -> 14% of each run, Pallas kernels for 20% -> 28%
where the time goes in v1:
time: 224 us; the launch traced here: 223 us
  Pallas kernels  81.9 us (37%)
  waiting for transfers between devices  51.7 us (23%)
  starting transfers between devices  45.2 us (20%)
  other arithmetic  23.4 us (10%)
  local copies, waits for them, and re-layouts  14.6 us (7%)
  matrix products  4.94 us (2%)
    ppermute x16, starting transfers between devices, ahead(): return lax.ppermute(block, 'dp', self.forward)  25.1 us
    pallas_call x10, Pallas kernels, ring_sum(): pl.pallas_call(kernel, out_shape=tuple((shape((planes, r, lanes), kind) f...  24.5 us
    pallas_call x4, Pallas kernels, weight_grads(): pl.pallas_call(outer_kernel, grid=(planes,), out_shape=shape((planes, cut...  19.1 us
    ppermute x16, waiting for transfers between devices, ahead(): return lax.ppermute(block, 'dp', self.forward)  16.5 us
    ppermute x16, waiting for transfers between devices, back(): return lax.ppermute(block, 'dp', self.backward)  16.3 us
    ppermute x8, waiting for transfers between devices, swap(): return lax.ppermute(block, 'tensor', [(0, 1), (1, 0)])  14.5 us
    pallas_call x1, Pallas kernels, back_call(): pl.pallas_call(back_kernel, out_shape=(shape((3, group, lanes), BF), shap...  11.7 us
    ppermute x8, starting transfers between devices, swap(): return lax.ppermute(block, 'tensor', [(0, 1), (1, 0)])  10.9 us
  transfers between devices with their start and end apart: 46, of which 23 were waited for; matrix products, arithmetic and copies ran while one was open for 14% of the time, Pallas kernels for 28%

profile of v1, /device:TPU:0, one launch (start us, length us, event | category | flops | bytes accessed | tf_op | source)
XLA Modules:
  0.0 223.1 jit_solution(10284230157247803863)
XLA Ops:
  3.3 3.1 %collective-permute-start.1 = (bf16[4,64,512]{2,1,0:T(8,128)(2,1)S(1)}, bf16[4,64,512]{2,1,0:T(8,128)(2,1)S(1)}, u32[]{:S(2)}, u32[]{:S(2)}) collective-permute-start(bf16[4,64,512]{2,1,0:T(8,128)(2,1)S(1)} %pad_maximum_fusion.4.refs_0_), channel_id=1, source_target_pairs={{0,8},{2,10},{8,16},{10,18},{16,24},{18,26},{24,28},{26,30},{28,20... | collective-permute-start | bytes 786440 | tf_op jit(solution)/shard_map/ppermute | solution.py:473
  9.0 2.0 collective-permute-start.7
  12.2 2.0 collective-permute-start
  17.4 2.8 %fusion.27 = (f32[256,512]{1,0:T(8,128)}, f32[256,512]{1,0:T(8,128)}) fusion(f32[512]{0:T(512)S(1)} %get-tuple-element.190, f32[512]{0:T(512)S(1)} %get-tuple-element.189, f32[256]{0:T(256)S(1)} %subtract_convert_fusion), kind=kLoop, calls=%fused_computation.41 | loop fusion | flops 262144 | bytes 1053696 | tf_op jit(solution)/shard_map/mul | solution.py:30
  20.3 9.5 %collective-permute-done.3.refs_3_ = bf16[4,64,512]{2,1,0:T(8,128)(2,1)S(1)} collective-permute-done((bf16[4,64,512]{2,1,0:T(8,128)(2,1)S(1)}, bf16[4,64,512]{2,1,0:T(8,128)(2,1)S(1)}, u32[]{:S(2)}, u32[]{:S(2)}) %collective-permute-start.3) | collective-permute-done | bytes 262176 | tf_op jit(solution)/shard_map/ppermute | solution.py:473
  36.2 2.3 %collective-permute-done.5.refs_0_ = bf16[4,64,512]{2,1,0:T(8,128)(2,1)S(1)} collective-permute-done((bf16[4,64,512]{2,1,0:T(8,128)(2,1)S(1)}, bf16[4,64,512]{2,1,0:T(8,128)(2,1)S(1)}, u32[]{:S(2)}, u32[]{:S(2)}) %collective-permute-start.5) | collective-permute-done | bytes 262176 | tf_op jit(solution)/shard_map/ppermute | solution.py:473
  43.1 2.1 stack_rows.4.refs_0_
  52.0 8.0 %attend.1 = (bf16[3,256,512]{2,1,0:T(8,128)(2,1)}, bf16[256,512]{1,0:T(8,128)(2,1)}, bf16[256,1024]{1,0:T(8,128)(2,1)}, f32[128,1024]{1,0:T(8,128)}, bf16[128,1024]{1,0:T(8,128)(2,1)}) custom-call(bf16[256,1024]{1,0:T(8,128)(2,1)} %pad_maximum_fusion.x, s32[256,1]{1,0:T(8,128)} %copy.24.docs, s32[1,256]{1,0:T(1,128)} %bitcast.44, ...), custom_call_target="tpu_custom_call" | custom-call | flops 1000 | bytes 1000 | tf_op jit(solution)/shard_map/attend/pallas_call | solution.py:184
  65.9 2.5 %collective-permute-done.13 = bf16[128,1024]{1,0:T(8,128)(2,1)S(1)} collective-permute-done((bf16[128,1024]{1,0:T(8,128)(2,1)}, bf16[128,1024]{1,0:T(8,128)(2,1)S(1)}, u32[]{:S(2)}, u32[]{:S(2)}) %collective-permute-start.13) | collective-permute-done | bytes 262176 | tf_op jit(solution)/shard_map/ppermute | solution.py:555
  72.4 5.7 %collective-permute-done.14 = bf16[128,1024]{1,0:T(8,128)(2,1)S(1)} collective-permute-done((bf16[128,1024]{1,0:T(8,128)(2,1)S(1)}, bf16[128,1024]{1,0:T(8,128)(2,1)S(1)}, u32[]{:S(2)}, u32[]{:S(2)}) %collective-permute-start.14) | collective-permute-done | bytes 262176 | tf_op jit(solution)/shard_map/ppermute | solution.py:555
  82.4 2.9 %stack_rows.6.refs_0_ = bf16[3,320,1408]{2,1,0:T(8,128)(2,1)} custom-call(bf16[3,64,1408]{2,1,0:T(8,128)(2,1)} %fusion.21.refs_0_, bf16[3,64,1408]{2,1,0:T(8,128)(2,1)S(1)} %copy-done.5, bf16[3,64,1408]{2,1,0:T(8,128)(2,1)S(1)} %copy-done.8, bf16[3,64,1408]{2,1,0:T(8,128)(2,1)} %collective-permute-done.15.refs_3_, ...), custom_call_target="tpu_custom_call" | custom-call | flops 99999997952 | bytes 1000000000 | tf_op jit(solution)/shard_map/stack_rows/pallas_call | solution.py:125
  86.3 2.4 %collective-permute-done.20.refs_3_ = bf16[3,32,1408]{2,1,0:T(8,128)(2,1)} collective-permute-done((bf16[3,32,1408]{2,1,0:T(8,128)(2,1)}, bf16[3,32,1408]{2,1,0:T(8,128)(2,1)}, u32[]{:S(2)}, u32[]{:S(2)}) %collective-permute-start.20) | collective-permute-done | bytes 270368 | tf_op jit(solution)/shard_map/ppermute | solution.py:476
  88.7 2.2 stack_rows.7.refs_1_
  91.0 3.7 %collective-permute-done.22.refs_3_ = bf16[3,192,1408]{2,1,0:T(8,128)(2,1)S(1)} collective-permute-done((bf16[3,192,1408]{2,1,0:T(8,128)(2,1)}, bf16[3,192,1408]{2,1,0:T(8,128)(2,1)S(1)}, u32[]{:S(2)}, u32[]{:S(2)}) %collective-permute-start.22) | collective-permute-done | bytes 1622048 | tf_op jit(solution)/shard_map/ppermute | solution.py:479
  95.9 10.4 %mlp.1 = (bf16[3,256,1408]{2,1,0:T(8,128)(2,1)}, f32[128,1024]{1,0:T(8,128)}, bf16[128,1024]{1,0:T(8,128)(2,1)}, f32[128,1024]{1,0:T(8,128)}, bf16[128,1024]{1,0:T(8,128)(2,1)}) custom-call(bf16[256,1024]{1,0:T(8,128)(2,1)} %pad_maximum_fusion.2.hat.first, bf16[256,1024]{1,0:T(8,128)(2,1)} %pad_maximum_fusion.1.cot.second, ...), custom_call_target="tpu_custom_call" | custom-call | flops 1000 | bytes 1000 | tf_op jit(solution)/shard_map/mlp/pallas_call | solution.py:241
  106.3 5.2 %weight_grads.4 = bf16[3,512,1408]{2,1,0:T(8,128)(2,1)} custom-call(bf16[256,1024]{1,0:T(8,128)(2,1)} %pad_maximum_fusion.2.hat.first, bf16[256,1024]{1,0:T(8,128)(2,1)} %pad_maximum_fusion.1.cot.second, bf16[3,256,1408]{2,1,0:T(8,128)(2,1)} %get-tuple-element.93.three.last, bf16[3,256,1408]{2,1,0:T(8,128)(2,1)} %get-tuple-element.93.three.last), custom_call_target="tpu_custom_call" | custom-call | flops 99999997952 | bytes 1000000000 | tf_op jit(solution)/shard_map/weight_grads/pallas_call | solution.py:337
  113.2 5.2 %weight_grads.5.refs_0_ = bf16[3,512,1408]{2,1,0:T(8,128)(2,1)} custom-call(bf16[256,1024]{1,0:T(8,128)(2,1)} %pad_maximum_fusion.2.hat.first, bf16[256,1024]{1,0:T(8,128)(2,1)} %pad_maximum_fusion.1.cot.second, bf16[3,256,1408]{2,1,0:T(8,128)(2,1)} %get-tuple-element.93.three.last, bf16[3,256,1408]{2,1,0:T(8,128)(2,1)} %get-tuple-element.93.three.last), custom_call_target="tpu_custom_call" | custom-call | flops 99999997952 | bytes 1000000000 | tf_op jit(solution)/shard_map/weight_grads/pallas_call | solution.py:337
  119.2 2.2 ring_first.2
  126.3 4.8 %collective-permute-done.25 = bf16[128,1024]{1,0:T(8,128)(2,1)S(1)} collective-permute-done((bf16[128,1024]{1,0:T(8,128)(2,1)S(1)}, bf16[128,1024]{1,0:T(8,128)(2,1)S(1)}, u32[]{:S(2)}, u32[]{:S(2)}) %collective-permute-start.25) | collective-permute-done | bytes 262176 | tf_op jit(solution)/shard_map/ppermute | solution.py:555
  132.7 2.6 %ring_middle.6 = (bf16[3,64,1408]{2,1,0:T(8,128)(2,1)}, bf16[3,64,1408]{2,1,0:T(8,128)(2,1)}) custom-call(bf16[3,512,1408]{2,1,0:T(8,128)(2,1)} %weight_grads.5.refs_0_, bf16[3,512,1408]{2,1,0:T(8,128)(2,1)} %collective-permute-done.24.refs_1_, bf16[3,32,1408]{2,1,0:T(8,128)(2,1)S(1)} %collective-permute-done.26.refs_2_, ...), custom_call_target="tpu_custom_call" | custom-call | flops 1000 | bytes 1000 | tf_op jit(solution)/shard_map/ring_middle/pallas_call | solution.py:385
  137.5 11.7 %attend_back.1 = (bf16[3,256,512]{2,1,0:T(8,128)(2,1)}, f32[128,1024]{1,0:T(8,128)}, bf16[128,1024]{1,0:T(8,128)(2,1)}) custom-call(bf16[256,1024]{1,0:T(8,128)(2,1)} %pad_maximum_fusion.3.grad.second, bf16[3,256,512]{2,1,0:T(8,128)(2,1)} %get-tuple-element.103.qkv, s32[256,1]{1,0:T(8,128)} %copy.24.docs, s32[1,256]{1,0:T(1,128)} %bitcast.45, ...), custom_call_target="tpu_custom_call" | custom-call | flops 1000 | bytes 1000 | tf_op jit(solution)/shard_map/attend_back/pallas_call | solution.py:290
  150.0 2.6 %ring_middle.7 = (bf16[3,64,1408]{2,1,0:T(8,128)(2,1)}, bf16[3,64,1408]{2,1,0:T(8,128)(2,1)}) custom-call(bf16[3,512,1408]{2,1,0:T(8,128)(2,1)} %weight_grads.5.refs_0_, bf16[3,512,1408]{2,1,0:T(8,128)(2,1)} %collective-permute-done.24.refs_1_, bf16[3,64,1408]{2,1,0:T(8,128)(2,1)S(1)} %collective-permute-done.30.refs_2_, ...), custom_call_target="tpu_custom_call" | custom-call | flops 1000 | bytes 1000 | tf_op jit(solution)/shard_map/ring_middle/pallas_call | solution.py:385
  154.7 4.3 %weight_grads.6 = bf16[4,512,512]{2,1,0:T(8,128)(2,1)} custom-call(bf16[256,1024]{1,0:T(8,128)(2,1)} %get-tuple-element.114.first, bf16[256,1024]{1,0:T(8,128)(2,1)} %pad_maximum_fusion.3.grad.second, bf16[3,256,512]{2,1,0:T(8,128)(2,1)} %get-tuple-element.112.three, bf16[256,512]{1,0:T(8,128)(2,1)} %get-tuple-element.113.last), custom_call_target="tpu_custom_call" | custom-call | flops 99999997952 | bytes 1000000000 | tf_op jit(solution)/shard_map/weight_grads/pallas_call | solution.py:337
  159.0 4.4 %weight_grads.7.refs_0_ = bf16[4,512,512]{2,1,0:T(8,128)(2,1)} custom-call(bf16[256,1024]{1,0:T(8,128)(2,1)} %get-tuple-element.114.first, bf16[256,1024]{1,0:T(8,128)(2,1)} %pad_maximum_fusion.3.grad.second, bf16[3,256,512]{2,1,0:T(8,128)(2,1)} %get-tuple-element.112.three, bf16[256,512]{1,0:T(8,128)(2,1)} %get-tuple-element.113.last), custom_call_target="tpu_custom_call" | custom-call | flops 99999997952 | bytes 1000000000 | tf_op jit(solution)/shard_map/weight_grads/pallas_call | solution.py:337
  163.4 2.1 ring_first.3
  168.9 3.8 %ring_middle.9 = (bf16[3,64,1408]{2,1,0:T(8,128)(2,1)}, bf16[3,64,1408]{2,1,0:T(8,128)(2,1)}) custom-call(bf16[3,512,1408]{2,1,0:T(8,128)(2,1)} %weight_grads.5.refs_0_, bf16[3,512,1408]{2,1,0:T(8,128)(2,1)} %collective-permute-done.24.refs_1_, bf16[3,64,1408]{2,1,0:T(8,128)(2,1)} %collective-permute-done.35.refs_2_, ...), custom_call_target="tpu_custom_call" | custom-call | flops 1000 | bytes 1000 | tf_op jit(solution)/shard_map/ring_middle/pallas_call | solution.py:385
  176.4 1.9 ring_middle.8
  185.6 6.8 %collective-permute-done.37.refs_2_ = bf16[4,64,512]{2,1,0:T(8,128)(2,1)S(1)} collective-permute-done((bf16[4,64,512]{2,1,0:T(8,128)(2,1)}, bf16[4,64,512]{2,1,0:T(8,128)(2,1)S(1)}, u32[]{:S(2)}, u32[]{:S(2)}) %collective-permute-start.37) | collective-permute-done | bytes 262176 | tf_op jit(solution)/shard_map/ppermute | solution.py:476
  192.6 1.9 ring_middle.10
  196.7 3.5 %ring_last.2 = f32[3,64,1408]{2,1,0:T(8,128)} custom-call(bf16[3,512,1408]{2,1,0:T(8,128)(2,1)} %weight_grads.5.refs_0_, bf16[3,512,1408]{2,1,0:T(8,128)(2,1)} %collective-permute-done.24.refs_1_, bf16[3,64,1408]{2,1,0:T(8,128)(2,1)S(1)} %collective-permute-done.41.refs_2_, bf16[3,64,1408]{2,1,0:T(8,128)(2,1)} %collective-permute-done.42.refs_3_), custom_call_target="tpu_custom_call" | custom-call | flops 1000 | bytes 1000 | tf_op jit(solution)/shard_map/ring_last/pallas_call | solution.py:385
  204.8 2.0 ring_middle.11
  208.9 2.9 %fusion.7 = bf16[128,1024]{1,0:T(8,128)(2,1)} fusion(s32[1024]{0:T(1024)S(1)} %copy-done.31, bf16[128,1024]{1,0:T(8,128)(2,1)} %collective-permute-done.29, f32[128,1024]{1,0:T(8,128)S(1)} %copy-done.11, f32[128,1024]{1,0:T(8,128)} %get-tuple-element.89), kind=kOutput, calls=%fused_computation.8 | convolution fusion | flops 270139392 | bytes 1576960 | tf_op jit(solution)/shard_map/te,de->td/dot_general | solution.py:48
  (223 shorter events, 92.0 us)
Async XLA Ops:
  3.3 11.8 %collective-permute-start.1 = (bf16[4,64,512]{2,1,0:T(8,128)(2,1)S(1)}, bf16[4,64,512]{2,1,0:T(8,128)(2,1)S(1)}, u32[]{:S(2)}, u32[]{:S(2)}) collective-permute-start(bf16[4,64,512]{2,1,0:T(8,128)(2,1)S(1)} %pad_maximum_fusion.4.refs_0_), channel_id=1, source_target_pairs={{0,8},{2,10},{8,16},{10,18},{16,24},{18,26},{24,28},{26,30},{28,20... | collective-permute-start | bytes 786440 | tf_op jit(solution)/shard_map/ppermute | solution.py:473
  6.4 9.0 %collective-permute-start.2 = (bf16[4,64,512]{2,1,0:T(8,128)(2,1)S(1)}, bf16[4,64,512]{2,1,0:T(8,128)(2,1)S(1)}, u32[]{:S(2)}, u32[]{:S(2)}) collective-permute-start(bf16[4,64,512]{2,1,0:T(8,128)(2,1)S(1)} %pad_maximum_fusion.4.refs_0_), channel_id=1, source_target_pairs={{0,4},{2,6},{8,0},{10,2},{16,8},{18,10},{24,16},{26,18},{28,24},{3... | collective-permute-start | bytes 786440 | tf_op jit(solution)/shard_map/ppermute | solution.py:476
  9.0 27.1 %collective-permute-start.7 = (bf16[3,64,1408]{2,1,0:T(8,128)(2,1)}, bf16[3,64,1408]{2,1,0:T(8,128)(2,1)S(1)}, u32[]{:S(2)}, u32[]{:S(2)}) collective-permute-start(bf16[3,64,1408]{2,1,0:T(8,128)(2,1)} %fusion.21.refs_0_), channel_id=1, source_target_pairs={{0,8},{2,10},{8,16},{10,18},{16,24},{18,26},{24,28},{26,30},{28,20... | collective-permute-start | bytes 1622024 | tf_op jit(solution)/shard_map/ppermute | solution.py:473
  11.1 25.1 %collective-permute-start.8 = (bf16[3,64,1408]{2,1,0:T(8,128)(2,1)}, bf16[3,64,1408]{2,1,0:T(8,128)(2,1)S(1)}, u32[]{:S(2)}, u32[]{:S(2)}) collective-permute-start(bf16[3,64,1408]{2,1,0:T(8,128)(2,1)} %fusion.21.refs_0_), channel_id=1, source_target_pairs={{0,4},{2,6},{8,0},{10,2},{16,8},{18,10},{24,16},{26,18},{28,24},{3... | collective-permute-start | bytes 1622024 | tf_op jit(solution)/shard_map/ppermute | solution.py:476
  12.2 21.2 %collective-permute-start = (bf16[256,1024]{1,0:T(8,128)(2,1)S(1)}, bf16[256,1024]{1,0:T(8,128)(2,1)}, u32[]{:S(2)}, u32[]{:S(2)}) collective-permute-start(bf16[256,1024]{1,0:T(8,128)(2,1)S(1)} %fusion.6), channel_id=1, source_target_pairs={{0,1},{1,0},{2,3},{3,2},{4,5},{5,4},{6,7},{7,6},{8,9},{9,8},{10,11... | collective-permute-start | bytes 1572872 | tf_op jit(solution)/shard_map/ppermute | solution.py:555
  15.4 14.4 %collective-permute-start.3 = (bf16[4,64,512]{2,1,0:T(8,128)(2,1)S(1)}, bf16[4,64,512]{2,1,0:T(8,128)(2,1)S(1)}, u32[]{:S(2)}, u32[]{:S(2)}) collective-permute-start(bf16[4,64,512]{2,1,0:T(8,128)(2,1)S(1)} %collective-permute-done.1.refs_1_), channel_id=1, source_target_pairs={{0,8},{2,10},{8,16},{10,18},{16,24},{18,26},{24,28},{26,30},{28,20... | collective-permute-start | bytes 786440 | tf_op jit(solution)/shard_map/ppermute | solution.py:473
  16.9 14.4 %collective-permute-start.4 = (bf16[4,64,512]{2,1,0:T(8,128)(2,1)S(1)}, bf16[4,64,512]{2,1,0:T(8,128)(2,1)S(1)}, u32[]{:S(2)}, u32[]{:S(2)}) collective-permute-start(bf16[4,64,512]{2,1,0:T(8,128)(2,1)S(1)} %collective-permute-done.2.refs_2_), channel_id=1, source_target_pairs={{0,4},{2,6},{8,0},{10,2},{16,8},{18,10},{24,16},{26,18},{28,24},{3... | collective-permute-start | bytes 786440 | tf_op jit(solution)/shard_map/ppermute | solution.py:476
  47.7 14.8 %collective-permute-start.15 = (bf16[3,64,1408]{2,1,0:T(8,128)(2,1)S(1)}, bf16[3,64,1408]{2,1,0:T(8,128)(2,1)}, u32[]{:S(2)}, u32[]{:S(2)}) collective-permute-start(bf16[3,64,1408]{2,1,0:T(8,128)(2,1)S(1)} %copy-done.4), channel_id=1, source_target_pairs={{0,8},{2,10},{8,16},{10,18},{16,24},{18,26},{24,28},{26,30},{28,20... | collective-permute-start | bytes 1622024 | tf_op jit(solution)/shard_map/ppermute | solution.py:473
  49.4 14.4 %collective-permute-start.16 = (bf16[3,64,1408]{2,1,0:T(8,128)(2,1)S(1)}, bf16[3,64,1408]{2,1,0:T(8,128)(2,1)}, u32[]{:S(2)}, u32[]{:S(2)}) collective-permute-start(bf16[3,64,1408]{2,1,0:T(8,128)(2,1)S(1)} %copy-done.7), channel_id=1, source_target_pairs={{0,4},{2,6},{8,0},{10,2},{16,8},{18,10},{24,16},{26,18},{28,24},{3... | collective-permute-start | bytes 1622024 | tf_op jit(solution)/shard_map/ppermute | solution.py:476
  60.0 8.4 %collective-permute-start.13 = (bf16[128,1024]{1,0:T(8,128)(2,1)}, bf16[128,1024]{1,0:T(8,128)(2,1)S(1)}, u32[]{:S(2)}, u32[]{:S(2)}) collective-permute-start(bf16[128,1024]{1,0:T(8,128)(2,1)} %get-tuple-element.81), channel_id=1, source_target_pairs={{0,1},{1,0},{2,3},{3,2},{4,5},{5,4},{6,7},{7,6},{8,9},{9,8},{10,11... | collective-permute-start | bytes 786440 | tf_op jit(solution)/shard_map/ppermute | solution.py:555
  63.8 15.1 %collective-permute-start.17 = (bf16[3,64,1408]{2,1,0:T(8,128)(2,1)}, bf16[3,64,1408]{2,1,0:T(8,128)(2,1)S(1)}, u32[]{:S(2)}, u32[]{:S(2)}) collective-permute-start(bf16[3,64,1408]{2,1,0:T(8,128)(2,1)} %collective-permute-done.15.refs_3_), channel_id=1, source_target_pairs={{0,8},{2,10},{8,16},{10,18},{16,24},{18,26},{24,28},{26,30},{28,20... | collective-permute-start | bytes 1622024 | tf_op jit(solution)/shard_map/ppermute | solution.py:473
  65.4 13.5 %collective-permute-start.18 = (bf16[3,64,1408]{2,1,0:T(8,128)(2,1)}, bf16[3,64,1408]{2,1,0:T(8,128)(2,1)S(1)}, u32[]{:S(2)}, u32[]{:S(2)}) collective-permute-start(bf16[3,64,1408]{2,1,0:T(8,128)(2,1)} %collective-permute-done.16.refs_4_), channel_id=1, source_target_pairs={{0,4},{2,6},{8,0},{10,2},{16,8},{18,10},{24,16},{26,18},{28,24},{3... | collective-permute-start | bytes 1622024 | tf_op jit(solution)/shard_map/ppermute | solution.py:476
  85.4 9.3 %collective-permute-start.21 = (bf16[3,320,1408]{2,1,0:T(8,128)(2,1)}, bf16[3,320,1408]{2,1,0:T(8,128)(2,1)}, u32[]{:S(2)}, u32[]{:S(2)}) collective-permute-start(bf16[3,320,1408]{2,1,0:T(8,128)(2,1)} %stack_rows.6.refs_0_), channel_id=1, source_target_pairs={{0,2},{2,0},{4,6},{6,4},{8,10},{10,8},{12,14},{14,12},{16,18},{18,... | collective-permute-start | bytes 8110088 | tf_op jit(solution)/shard_map/ppermute | solution.py:479
  111.5 7.7 %collective-permute-start.24 = (bf16[3,512,1408]{2,1,0:T(8,128)(2,1)}, bf16[3,512,1408]{2,1,0:T(8,128)(2,1)}, u32[]{:S(2)}, u32[]{:S(2)}) collective-permute-start(bf16[3,512,1408]{2,1,0:T(8,128)(2,1)} %weight_grads.4), channel_id=1, source_target_pairs={{0,2},{2,0},{4,6},{6,4},{8,10},{10,8},{12,14},{14,12},{16,18},{18,... | collective-permute-start | bytes 12976136 | tf_op jit(solution)/shard_map/ppermute | solution.py:479
  111.7 9.7 %collective-permute-start.23 = (bf16[128,1024]{1,0:T(8,128)(2,1)S(1)}, bf16[128,1024]{1,0:T(8,128)(2,1)S(1)}, u32[]{:S(2)}, u32[]{:S(2)}) collective-permute-start(bf16[128,1024]{1,0:T(8,128)(2,1)S(1)} %copy-done.42), channel_id=1, source_target_pairs={{0,1},{1,0},{2,3},{3,2},{4,5},{5,4},{6,7},{7,6},{8,9},{9,8},{10,11... | collective-permute-start | bytes 786440 | tf_op jit(solution)/shard_map/ppermute | solution.py:555
  122.8 8.3 %collective-permute-start.25 = (bf16[128,1024]{1,0:T(8,128)(2,1)S(1)}, bf16[128,1024]{1,0:T(8,128)(2,1)S(1)}, u32[]{:S(2)}, u32[]{:S(2)}) collective-permute-start(bf16[128,1024]{1,0:T(8,128)(2,1)S(1)} %get-tuple-element.170), channel_id=1, source_target_pairs={{0,1},{1,0},{2,3},{3,2},{4,5},{5,4},{6,7},{7,6},{8,9},{9,8},{10,11... | collective-permute-start | bytes 786440 | tf_op jit(solution)/shard_map/ppermute | solution.py:555
  124.3 8.2 %collective-permute-start.26 = (bf16[3,32,1408]{2,1,0:T(8,128)(2,1)S(1)}, bf16[3,32,1408]{2,1,0:T(8,128)(2,1)S(1)}, u32[]{:S(2)}, u32[]{:S(2)}) collective-permute-start(bf16[3,32,1408]{2,1,0:T(8,128)(2,1)S(1)} %copy-done.38), channel_id=1, source_target_pairs={{0,4},{2,6},{8,0},{10,2},{16,8},{18,10},{24,16},{26,18},{28,24},{3... | collective-permute-start | bytes 811016 | tf_op jit(solution)/shard_map/ppermute | solution.py:476
  124.8 8.0 %collective-permute-start.27 = (bf16[3,32,1408]{2,1,0:T(8,128)(2,1)S(1)}, bf16[3,32,1408]{2,1,0:T(8,128)(2,1)S(1)}, u32[]{:S(2)}, u32[]{:S(2)}) collective-permute-start(bf16[3,32,1408]{2,1,0:T(8,128)(2,1)S(1)} %copy-done.37), channel_id=1, source_target_pairs={{0,8},{2,10},{8,16},{10,18},{16,24},{18,26},{24,28},{26,30},{28,20... | collective-permute-start | bytes 811016 | tf_op jit(solution)/shard_map/ppermute | solution.py:473
  135.4 14.6 %collective-permute-start.30 = (bf16[3,64,1408]{2,1,0:T(8,128)(2,1)}, bf16[3,64,1408]{2,1,0:T(8,128)(2,1)S(1)}, u32[]{:S(2)}, u32[]{:S(2)}) collective-permute-start(bf16[3,64,1408]{2,1,0:T(8,128)(2,1)} %get-tuple-element.100), channel_id=1, source_target_pairs={{0,4},{2,6},{8,0},{10,2},{16,8},{18,10},{24,16},{26,18},{28,24},{3... | collective-permute-start | bytes 1622024 | tf_op jit(solution)/shard_map/ppermute | solution.py:476
  135.9 14.1 %collective-permute-start.31 = (bf16[3,64,1408]{2,1,0:T(8,128)(2,1)}, bf16[3,64,1408]{2,1,0:T(8,128)(2,1)S(1)}, u32[]{:S(2)}, u32[]{:S(2)}) collective-permute-start(bf16[3,64,1408]{2,1,0:T(8,128)(2,1)} %get-tuple-element.101), channel_id=1, source_target_pairs={{0,8},{2,10},{8,16},{10,18},{16,24},{18,26},{24,28},{26,30},{28,20... | collective-permute-start | bytes 1622024 | tf_op jit(solution)/shard_map/ppermute | solution.py:473
  149.1 18.4 %collective-permute-start.28 = (bf16[128,1024]{1,0:T(8,128)(2,1)}, bf16[128,1024]{1,0:T(8,128)(2,1)}, u32[]{:S(2)}, u32[]{:S(2)}) collective-permute-start(bf16[128,1024]{1,0:T(8,128)(2,1)} %get-tuple-element.104), channel_id=1, source_target_pairs={{0,1},{1,0},{2,3},{3,2},{4,5},{5,4},{6,7},{7,6},{8,9},{9,8},{10,11... | collective-permute-start | bytes 786440 | tf_op jit(solution)/shard_map/ppermute | solution.py:555
  152.6 16.3 %collective-permute-start.35 = (bf16[3,64,1408]{2,1,0:T(8,128)(2,1)}, bf16[3,64,1408]{2,1,0:T(8,128)(2,1)}, u32[]{:S(2)}, u32[]{:S(2)}) collective-permute-start(bf16[3,64,1408]{2,1,0:T(8,128)(2,1)} %get-tuple-element.109), channel_id=1, source_target_pairs={{0,4},{2,6},{8,0},{10,2},{16,8},{18,10},{24,16},{26,18},{28,24},{3... | collective-permute-start | bytes 1622024 | tf_op jit(solution)/shard_map/ppermute | solution.py:476
  153.1 15.8 %collective-permute-start.36 = (bf16[3,64,1408]{2,1,0:T(8,128)(2,1)}, bf16[3,64,1408]{2,1,0:T(8,128)(2,1)}, u32[]{:S(2)}, u32[]{:S(2)}) collective-permute-start(bf16[3,64,1408]{2,1,0:T(8,128)(2,1)} %get-tuple-element.110), channel_id=1, source_target_pairs={{0,8},{2,10},{8,16},{10,18},{16,24},{18,26},{24,28},{26,30},{28,20... | collective-permute-start | bytes 1622024 | tf_op jit(solution)/shard_map/ppermute | solution.py:473
  165.5 9.4 %collective-permute-start.33 = (bf16[4,32,512]{2,1,0:T(8,128)(2,1)}, bf16[4,32,512]{2,1,0:T(8,128)(2,1)S(1)}, u32[]{:S(2)}, u32[]{:S(2)}) collective-permute-start(bf16[4,32,512]{2,1,0:T(8,128)(2,1)} %get-tuple-element.115), channel_id=1, source_target_pairs={{0,4},{2,6},{8,0},{10,2},{16,8},{18,10},{24,16},{26,18},{28,24},{3... | collective-permute-start | bytes 393224 | tf_op jit(solution)/shard_map/ppermute | solution.py:476
  166.0 8.9 %collective-permute-start.34 = (bf16[4,32,512]{2,1,0:T(8,128)(2,1)}, bf16[4,32,512]{2,1,0:T(8,128)(2,1)S(1)}, u32[]{:S(2)}, u32[]{:S(2)}) collective-permute-start(bf16[4,32,512]{2,1,0:T(8,128)(2,1)} %get-tuple-element.116), channel_id=1, source_target_pairs={{0,8},{2,10},{8,16},{10,18},{16,24},{18,26},{24,28},{26,30},{28,20... | collective-permute-start | bytes 393224 | tf_op jit(solution)/shard_map/ppermute | solution.py:473
  167.6 41.4 %collective-permute-start.29 = (bf16[128,1024]{1,0:T(8,128)(2,1)S(1)}, bf16[128,1024]{1,0:T(8,128)(2,1)}, u32[]{:S(2)}, u32[]{:S(2)}) collective-permute-start(bf16[128,1024]{1,0:T(8,128)(2,1)S(1)} %copy-done.41), channel_id=1, source_target_pairs={{0,1},{1,0},{2,3},{3,2},{4,5},{5,4},{6,7},{7,6},{8,9},{9,8},{10,11... | collective-permute-start | bytes 786440 | tf_op jit(solution)/shard_map/ppermute | solution.py:555
  172.7 23.9 %collective-permute-start.41 = (bf16[3,64,1408]{2,1,0:T(8,128)(2,1)}, bf16[3,64,1408]{2,1,0:T(8,128)(2,1)S(1)}, u32[]{:S(2)}, u32[]{:S(2)}) collective-permute-start(bf16[3,64,1408]{2,1,0:T(8,128)(2,1)} %get-tuple-element.121), channel_id=1, source_target_pairs={{0,4},{2,6},{8,0},{10,2},{16,8},{18,10},{24,16},{26,18},{28,24},{3... | collective-permute-start | bytes 1622024 | tf_op jit(solution)/shard_map/ppermute | solution.py:476
  173.3 23.4 %collective-permute-start.42 = (bf16[3,64,1408]{2,1,0:T(8,128)(2,1)}, bf16[3,64,1408]{2,1,0:T(8,128)(2,1)}, u32[]{:S(2)}, u32[]{:S(2)}) collective-permute-start(bf16[3,64,1408]{2,1,0:T(8,128)(2,1)} %get-tuple-element.122), channel_id=1, source_target_pairs={{0,8},{2,10},{8,16},{10,18},{16,24},{18,26},{24,28},{26,30},{28,20... | collective-permute-start | bytes 1622024 | tf_op jit(solution)/shard_map/ppermute | solution.py:473
  178.4 14.1 %collective-permute-start.37 = (bf16[4,64,512]{2,1,0:T(8,128)(2,1)}, bf16[4,64,512]{2,1,0:T(8,128)(2,1)S(1)}, u32[]{:S(2)}, u32[]{:S(2)}) collective-permute-start(bf16[4,64,512]{2,1,0:T(8,128)(2,1)} %get-tuple-element.123), channel_id=1, source_target_pairs={{0,4},{2,6},{8,0},{10,2},{16,8},{18,10},{24,16},{26,18},{28,24},{3... | collective-permute-start | bytes 786440 | tf_op jit(solution)/shard_map/ppermute | solution.py:476
  178.9 13.7 %collective-permute-start.38 = (bf16[4,64,512]{2,1,0:T(8,128)(2,1)}, bf16[4,64,512]{2,1,0:T(8,128)(2,1)S(1)}, u32[]{:S(2)}, u32[]{:S(2)}) collective-permute-start(bf16[4,64,512]{2,1,0:T(8,128)(2,1)} %get-tuple-element.124), channel_id=1, source_target_pairs={{0,8},{2,10},{8,16},{10,18},{16,24},{18,26},{24,28},{26,30},{28,20... | collective-permute-start | bytes 786440 | tf_op jit(solution)/shard_map/ppermute | solution.py:473
  194.6 10.2 %collective-permute-start.39 = (bf16[4,64,512]{2,1,0:T(8,128)(2,1)}, bf16[4,64,512]{2,1,0:T(8,128)(2,1)S(1)}, u32[]{:S(2)}, u32[]{:S(2)}) collective-permute-start(bf16[4,64,512]{2,1,0:T(8,128)(2,1)} %get-tuple-element.129), channel_id=1, source_target_pairs={{0,4},{2,6},{8,0},{10,2},{16,8},{18,10},{24,16},{26,18},{28,24},{3... | collective-permute-start | bytes 786440 | tf_op jit(solution)/shard_map/ppermute | solution.py:476
  196.1 8.7 %collective-permute-start.40 = (bf16[4,64,512]{2,1,0:T(8,128)(2,1)}, bf16[4,64,512]{2,1,0:T(8,128)(2,1)S(1)}, u32[]{:S(2)}, u32[]{:S(2)}) collective-permute-start(bf16[4,64,512]{2,1,0:T(8,128)(2,1)} %get-tuple-element.130), channel_id=1, source_target_pairs={{0,8},{2,10},{8,16},{10,18},{16,24},{18,26},{24,28},{26,30},{28,20... | collective-permute-start | bytes 786440 | tf_op jit(solution)/shard_map/ppermute | solution.py:473
  (58 other events, 309.9 us)

commit v2 on v1

--- a/solution.py
+++ b/solution.py
@@ -634,7 +634,6 @@
     reduce_a.step()
     reduce_b.step(*reduce_a.sent)
     reduce_a.step(*reduce_b.sent)
-    raw_b = reduce_b.done(*reduce_a.sent)
 
     grad_hat_one = part + tie(swapped, *reduce_a.sent).astype(F32)
     grad_input = grad_residual + norm_back(grad_hat_one, normed_one, factor_one)
@@ -644,15 +643,16 @@
     spread = ein("te,de->td", parts, chosen)
     grad_input = spread[:count] + spread[count : 2 * count] + spread[2 * count :]
     out_swapped = swap(tie(out_away, swapped))
-    reduce_a.step(grad_input)
-
+    output = (residual + out_part + tie(out_swapped, *reduce_a.sent).astype(F32)).astype(BF)
+    output = ein("te,de->td", output, chosen).astype(BF)
+    reduce_a.step(grad_input, output)
+
+    raw_b = reduce_b.done(*reduce_a.sent)
+    reduce_a.step(raw_b)
     raw_b = tie(raw_b, *reduce_a.sent)[:, :, :hidden]
     grad_in = jnp.transpose(raw_b[:2] * gain_two[None, :, None], (1, 0, 2))
     grad_mo = raw_b[2].T
     gain_two_sum = jnp.sum(plain_in * raw_b[:2], axis=(0, 2))
-    reduce_a.step(grad_in, grad_mo, gain_two_sum)
-    output = (residual + out_part + tie(out_swapped, *reduce_a.sent).astype(F32)).astype(BF)
-    output = ein("te,de->td", output, chosen).astype(BF)
     raw_a = reduce_a.done()
 
     gain_sums = jnp.stack(

time: 224 us -> 223 us (level)
  waiting for transfers between devices: 51.7 us -> 47.3 us
    ppermute x16, waiting for transfers between devices: 16.3 us -> 13.5 us  [back(): return lax.ppermute(block, 'dp', self.backward)]
    unnamed x89 -> x85, local copies, waits for them, and re-layouts: 6.02 us -> 7.68 us
  transfers between devices with their start and end apart: 46 -> 46, of which waited for: 23 -> 25; matrix products, arithmetic and copies ran while one was open for 14% -> 14% of each run, Pallas kernels for 28% -> 27%
where the time goes in v2:
time: 223 us; the launch traced here: 222 us
  Pallas kernels  81.7 us (37%)
  waiting for transfers between devices  47.3 us (21%)
  starting transfers between devices  45.4 us (20%)
  other arithmetic  24.3 us (11%)
  local copies, waits for them, and re-layouts  16 us (7%)
  matrix products  5.56 us (2%)
    ppermute x16, starting transfers between devices, ahead(): return lax.ppermute(block, 'dp', self.forward)  24.9 us
    pallas_call x10, Pallas kernels, ring_sum(): pl.pallas_call(kernel, out_shape=tuple((shape((planes, r, lanes), kind) f...  24.6 us
    pallas_call x4, Pallas kernels, weight_grads(): pl.pallas_call(outer_kernel, grid=(planes,), out_shape=shape((planes, cut...  18.9 us
    ppermute x16, waiting for transfers between devices, ahead(): return lax.ppermute(block, 'dp', self.forward)  15.2 us
    ppermute x8, waiting for transfers between devices, swap(): return lax.ppermute(block, 'tensor', [(0, 1), (1, 0)])  14 us
    ppermute x16, waiting for transfers between devices, back(): return lax.ppermute(block, 'dp', self.backward)  13.5 us
    pallas_call x1, Pallas kernels, back_call(): pl.pallas_call(back_kernel, out_shape=(shape((3, group, lanes), BF), shap...  11.7 us
    ppermute x8, starting transfers between devices, swap(): return lax.ppermute(block, 'tensor', [(0, 1), (1, 0)])  10.9 us
  transfers between devices with their start and end apart: 46, of which 25 were waited for; matrix products, arithmetic and copies ran while one was open for 14% of the time, Pallas kernels for 27%

profile of v2, /device:TPU:0, one launch (start us, length us, event | category | flops | bytes accessed | tf_op | source)
XLA Modules:
  0.0 221.6 jit_solution(2483037309976327925)
XLA Ops:
  3.3 3.1 %collective-permute-start.1 = (bf16[4,64,512]{2,1,0:T(8,128)(2,1)S(1)}, bf16[4,64,512]{2,1,0:T(8,128)(2,1)S(1)}, u32[]{:S(2)}, u32[]{:S(2)}) collective-permute-start(bf16[4,64,512]{2,1,0:T(8,128)(2,1)S(1)} %pad_maximum_fusion.4.refs_0_), channel_id=1, source_target_pairs={{0,8},{2,10},{8,16},{10,18},{16,24},{18,26},{24,28},{26,30},{28,20... | collective-permute-start | bytes 786440 | tf_op jit(solution)/shard_map/ppermute | solution.py:473
  8.3 2.1 collective-permute-start.7
  12.2 2.0 collective-permute-start
  17.6 2.8 %fusion.27 = (f32[256,512]{1,0:T(8,128)}, f32[256,512]{1,0:T(8,128)}) fusion(f32[512]{0:T(512)S(1)} %get-tuple-element.190, f32[512]{0:T(512)S(1)} %get-tuple-element.189, f32[256]{0:T(256)S(1)} %subtract_convert_fusion), kind=kLoop, calls=%fused_computation.41 | loop fusion | flops 262144 | bytes 1053696 | tf_op jit(solution)/shard_map/mul | solution.py:30
  21.5 8.3 %collective-permute-done.3.refs_3_ = bf16[4,64,512]{2,1,0:T(8,128)(2,1)S(1)} collective-permute-done((bf16[4,64,512]{2,1,0:T(8,128)(2,1)S(1)}, bf16[4,64,512]{2,1,0:T(8,128)(2,1)S(1)}, u32[]{:S(2)}, u32[]{:S(2)}) %collective-permute-start.3) | collective-permute-done | bytes 262176 | tf_op jit(solution)/shard_map/ppermute | solution.py:473
  36.2 2.0 collective-permute-done.5.refs_0_
  41.7 2.1 stack_rows.4.refs_0_
  49.9 8.0 %attend.1 = (bf16[3,256,512]{2,1,0:T(8,128)(2,1)}, bf16[256,512]{1,0:T(8,128)(2,1)}, bf16[256,1024]{1,0:T(8,128)(2,1)}, f32[128,1024]{1,0:T(8,128)}, bf16[128,1024]{1,0:T(8,128)(2,1)}) custom-call(bf16[256,1024]{1,0:T(8,128)(2,1)} %pad_maximum_fusion.x, s32[256,1]{1,0:T(8,128)} %copy.24.docs, s32[1,256]{1,0:T(1,128)} %bitcast.44, ...), custom_call_target="tpu_custom_call" | custom-call | flops 1000 | bytes 1000 | tf_op jit(solution)/shard_map/attend/pallas_call | solution.py:184
  64.2 2.0 collective-permute-done.13
  70.3 5.7 %collective-permute-done.14 = bf16[128,1024]{1,0:T(8,128)(2,1)S(1)} collective-permute-done((bf16[128,1024]{1,0:T(8,128)(2,1)S(1)}, bf16[128,1024]{1,0:T(8,128)(2,1)S(1)}, u32[]{:S(2)}, u32[]{:S(2)}) %collective-permute-start.14) | collective-permute-done | bytes 262176 | tf_op jit(solution)/shard_map/ppermute | solution.py:555
  80.7 2.9 %stack_rows.6.refs_0_ = bf16[3,320,1408]{2,1,0:T(8,128)(2,1)} custom-call(bf16[3,64,1408]{2,1,0:T(8,128)(2,1)} %copy-done.17, bf16[3,64,1408]{2,1,0:T(8,128)(2,1)S(1)} %copy-done.5, bf16[3,64,1408]{2,1,0:T(8,128)(2,1)S(1)} %copy-done.8, bf16[3,64,1408]{2,1,0:T(8,128)(2,1)} %collective-permute-done.15.refs_3_, ...), custom_call_target="tpu_custom_call" | custom-call | flops 99999997952 | bytes 1000000000 | tf_op jit(solution)/shard_map/stack_rows/pallas_call | solution.py:125
  84.6 2.3 %collective-permute-done.20.refs_3_ = bf16[3,32,1408]{2,1,0:T(8,128)(2,1)} collective-permute-done((bf16[3,32,1408]{2,1,0:T(8,128)(2,1)}, bf16[3,32,1408]{2,1,0:T(8,128)(2,1)}, u32[]{:S(2)}, u32[]{:S(2)}) %collective-permute-start.20) | collective-permute-done | bytes 270368 | tf_op jit(solution)/shard_map/ppermute | solution.py:476
  86.9 2.2 stack_rows.7.refs_1_
  89.2 3.7 %collective-permute-done.22.refs_3_ = bf16[3,192,1408]{2,1,0:T(8,128)(2,1)S(1)} collective-permute-done((bf16[3,192,1408]{2,1,0:T(8,128)(2,1)}, bf16[3,192,1408]{2,1,0:T(8,128)(2,1)S(1)}, u32[]{:S(2)}, u32[]{:S(2)}) %collective-permute-start.22) | collective-permute-done | bytes 1622048 | tf_op jit(solution)/shard_map/ppermute | solution.py:479
  94.0 10.4 %mlp.1 = (bf16[3,256,1408]{2,1,0:T(8,128)(2,1)}, f32[128,1024]{1,0:T(8,128)}, bf16[128,1024]{1,0:T(8,128)(2,1)}, f32[128,1024]{1,0:T(8,128)}, bf16[128,1024]{1,0:T(8,128)(2,1)}) custom-call(bf16[256,1024]{1,0:T(8,128)(2,1)} %pad_maximum_fusion.2.hat.first, bf16[256,1024]{1,0:T(8,128)(2,1)} %pad_maximum_fusion.1.cot.second, ...), custom_call_target="tpu_custom_call" | custom-call | flops 1000 | bytes 1000 | tf_op jit(solution)/shard_map/mlp/pallas_call | solution.py:241
  104.5 5.2 %weight_grads.4 = bf16[3,512,1408]{2,1,0:T(8,128)(2,1)} custom-call(bf16[256,1024]{1,0:T(8,128)(2,1)} %pad_maximum_fusion.2.hat.first, bf16[256,1024]{1,0:T(8,128)(2,1)} %pad_maximum_fusion.1.cot.second, bf16[3,256,1408]{2,1,0:T(8,128)(2,1)} %get-tuple-element.93.three.last, bf16[3,256,1408]{2,1,0:T(8,128)(2,1)} %get-tuple-element.93.three.last), custom_call_target="tpu_custom_call" | custom-call | flops 99999997952 | bytes 1000000000 | tf_op jit(solution)/shard_map/weight_grads/pallas_call | solution.py:337
  111.4 5.1 %weight_grads.5.refs_0_ = bf16[3,512,1408]{2,1,0:T(8,128)(2,1)} custom-call(bf16[256,1024]{1,0:T(8,128)(2,1)} %pad_maximum_fusion.2.hat.first, bf16[256,1024]{1,0:T(8,128)(2,1)} %pad_maximum_fusion.1.cot.second, bf16[3,256,1408]{2,1,0:T(8,128)(2,1)} %get-tuple-element.93.three.last, bf16[3,256,1408]{2,1,0:T(8,128)(2,1)} %get-tuple-element.93.three.last), custom_call_target="tpu_custom_call" | custom-call | flops 99999997952 | bytes 1000000000 | tf_op jit(solution)/shard_map/weight_grads/pallas_call | solution.py:337
  117.4 2.2 ring_first.2
  119.9 2.0 fusion.80
  125.4 4.8 %collective-permute-done.25 = bf16[128,1024]{1,0:T(8,128)(2,1)S(1)} collective-permute-done((bf16[128,1024]{1,0:T(8,128)(2,1)S(1)}, bf16[128,1024]{1,0:T(8,128)(2,1)S(1)}, u32[]{:S(2)}, u32[]{:S(2)}) %collective-permute-start.25) | collective-permute-done | bytes 262176 | tf_op jit(solution)/shard_map/ppermute | solution.py:555
  131.9 2.7 %ring_middle.6 = (bf16[3,64,1408]{2,1,0:T(8,128)(2,1)}, bf16[3,64,1408]{2,1,0:T(8,128)(2,1)}) custom-call(bf16[3,512,1408]{2,1,0:T(8,128)(2,1)} %weight_grads.5.refs_0_, bf16[3,512,1408]{2,1,0:T(8,128)(2,1)} %collective-permute-done.24.refs_1_, bf16[3,32,1408]{2,1,0:T(8,128)(2,1)S(1)} %collective-permute-done.26.refs_2_, ...), custom_call_target="tpu_custom_call" | custom-call | flops 1000 | bytes 1000 | tf_op jit(solution)/shard_map/ring_middle/pallas_call | solution.py:385
  136.7 11.7 %attend_back.1 = (bf16[3,256,512]{2,1,0:T(8,128)(2,1)}, f32[128,1024]{1,0:T(8,128)}, bf16[128,1024]{1,0:T(8,128)(2,1)}) custom-call(bf16[256,1024]{1,0:T(8,128)(2,1)} %pad_maximum_fusion.3.grad.second, bf16[3,256,512]{2,1,0:T(8,128)(2,1)} %get-tuple-element.103.qkv, s32[256,1]{1,0:T(8,128)} %copy.24.docs, s32[1,256]{1,0:T(1,128)} %bitcast.45, ...), custom_call_target="tpu_custom_call" | custom-call | flops 1000 | bytes 1000 | tf_op jit(solution)/shard_map/attend_back/pallas_call | solution.py:290
  149.1 2.6 %ring_middle.7 = (bf16[3,64,1408]{2,1,0:T(8,128)(2,1)}, bf16[3,64,1408]{2,1,0:T(8,128)(2,1)}) custom-call(bf16[3,512,1408]{2,1,0:T(8,128)(2,1)} %weight_grads.5.refs_0_, bf16[3,512,1408]{2,1,0:T(8,128)(2,1)} %collective-permute-done.24.refs_1_, bf16[3,64,1408]{2,1,0:T(8,128)(2,1)S(1)} %collective-permute-done.30.refs_2_, ...), custom_call_target="tpu_custom_call" | custom-call | flops 1000 | bytes 1000 | tf_op jit(solution)/shard_map/ring_middle/pallas_call | solution.py:385
  153.8 4.3 %weight_grads.6 = bf16[4,512,512]{2,1,0:T(8,128)(2,1)} custom-call(bf16[256,1024]{1,0:T(8,128)(2,1)} %get-tuple-element.114.first, bf16[256,1024]{1,0:T(8,128)(2,1)} %pad_maximum_fusion.3.grad.second, bf16[3,256,512]{2,1,0:T(8,128)(2,1)} %get-tuple-element.112.three, bf16[256,512]{1,0:T(8,128)(2,1)} %get-tuple-element.113.last), custom_call_target="tpu_custom_call" | custom-call | flops 99999997952 | bytes 1000000000 | tf_op jit(solution)/shard_map/weight_grads/pallas_call | solution.py:337
  158.1 4.3 %weight_grads.7.refs_0_ = bf16[4,512,512]{2,1,0:T(8,128)(2,1)} custom-call(bf16[256,1024]{1,0:T(8,128)(2,1)} %get-tuple-element.114.first, bf16[256,1024]{1,0:T(8,128)(2,1)} %pad_maximum_fusion.3.grad.second, bf16[3,256,512]{2,1,0:T(8,128)(2,1)} %get-tuple-element.112.three, bf16[256,512]{1,0:T(8,128)(2,1)} %get-tuple-element.113.last), custom_call_target="tpu_custom_call" | custom-call | flops 99999997952 | bytes 1000000000 | tf_op jit(solution)/shard_map/weight_grads/pallas_call | solution.py:337
  162.5 2.1 ring_first.3
  168.1 3.8 %ring_middle.9 = (bf16[3,64,1408]{2,1,0:T(8,128)(2,1)}, bf16[3,64,1408]{2,1,0:T(8,128)(2,1)}) custom-call(bf16[3,512,1408]{2,1,0:T(8,128)(2,1)} %weight_grads.5.refs_0_, bf16[3,512,1408]{2,1,0:T(8,128)(2,1)} %collective-permute-done.24.refs_1_, bf16[3,64,1408]{2,1,0:T(8,128)(2,1)} %collective-permute-done.35.refs_2_, ...), custom_call_target="tpu_custom_call" | custom-call | flops 1000 | bytes 1000 | tf_op jit(solution)/shard_map/ring_middle/pallas_call | solution.py:385
  175.6 1.9 ring_middle.8
  185.3 2.7 %fusion.7 = bf16[128,1024]{1,0:T(8,128)(2,1)} fusion(s32[1024]{0:T(1024)S(1)} %copy-done.28, bf16[128,1024]{1,0:T(8,128)(2,1)} %collective-permute-done.29, f32[128,1024]{1,0:T(8,128)S(1)} %copy-done.11, f32[128,1024]{1,0:T(8,128)S(1)} %copy-done.34), kind=kOutput, calls=%fused_computation.8 | convolution fusion | flops 270139392 | bytes 1576960 | tf_op jit(solution)/shard_map/te,de->td/dot_general | solution.py:48
  188.0 3.6 %collective-permute-done.37.refs_2_ = bf16[4,64,512]{2,1,0:T(8,128)(2,1)S(1)} collective-permute-done((bf16[4,64,512]{2,1,0:T(8,128)(2,1)}, bf16[4,64,512]{2,1,0:T(8,128)(2,1)S(1)}, u32[]{:S(2)}, u32[]{:S(2)}) %collective-permute-start.37) | collective-permute-done | bytes 262176 | tf_op jit(solution)/shard_map/ppermute | solution.py:476
  195.9 3.5 %ring_last.2 = f32[3,64,1408]{2,1,0:T(8,128)} custom-call(bf16[3,512,1408]{2,1,0:T(8,128)(2,1)} %weight_grads.5.refs_0_, bf16[3,512,1408]{2,1,0:T(8,128)(2,1)} %collective-permute-done.24.refs_1_, bf16[3,64,1408]{2,1,0:T(8,128)(2,1)S(1)} %collective-permute-done.41.refs_2_, bf16[3,64,1408]{2,1,0:T(8,128)(2,1)} %collective-permute-done.42.refs_3_), custom_call_target="tpu_custom_call" | custom-call | flops 1000 | bytes 1000 | tf_op jit(solution)/shard_map/ring_last/pallas_call | solution.py:385
  203.3 1.9 ring_middle.11
  (219 shorter events, 96.1 us)
Async XLA Ops:
  3.3 11.8 %collective-permute-start.1 = (bf16[4,64,512]{2,1,0:T(8,128)(2,1)S(1)}, bf16[4,64,512]{2,1,0:T(8,128)(2,1)S(1)}, u32[]{:S(2)}, u32[]{:S(2)}) collective-permute-start(bf16[4,64,512]{2,1,0:T(8,128)(2,1)S(1)} %pad_maximum_fusion.4.refs_0_), channel_id=1, source_target_pairs={{0,8},{2,10},{8,16},{10,18},{16,24},{18,26},{24,28},{26,30},{28,20... | collective-permute-start | bytes 786440 | tf_op jit(solution)/shard_map/ppermute | solution.py:473
  6.4 9.2 %collective-permute-start.2 = (bf16[4,64,512]{2,1,0:T(8,128)(2,1)S(1)}, bf16[4,64,512]{2,1,0:T(8,128)(2,1)S(1)}, u32[]{:S(2)}, u32[]{:S(2)}) collective-permute-start(bf16[4,64,512]{2,1,0:T(8,128)(2,1)S(1)} %pad_maximum_fusion.4.refs_0_), channel_id=1, source_target_pairs={{0,4},{2,6},{8,0},{10,2},{16,8},{18,10},{24,16},{26,18},{28,24},{3... | collective-permute-start | bytes 786440 | tf_op jit(solution)/shard_map/ppermute | solution.py:476
  8.3 27.9 %collective-permute-start.7 = (bf16[3,64,1408]{2,1,0:T(8,128)(2,1)S(1)}, bf16[3,64,1408]{2,1,0:T(8,128)(2,1)S(1)}, u32[]{:S(2)}, u32[]{:S(2)}) collective-permute-start(bf16[3,64,1408]{2,1,0:T(8,128)(2,1)S(1)} %fusion.21.refs_0_), channel_id=1, source_target_pairs={{0,8},{2,10},{8,16},{10,18},{16,24},{18,26},{24,28},{26,30},{28,20... | collective-permute-start | bytes 1622024 | tf_op jit(solution)/shard_map/ppermute | solution.py:473
  10.3 25.8 %collective-permute-start.8 = (bf16[3,64,1408]{2,1,0:T(8,128)(2,1)S(1)}, bf16[3,64,1408]{2,1,0:T(8,128)(2,1)S(1)}, u32[]{:S(2)}, u32[]{:S(2)}) collective-permute-start(bf16[3,64,1408]{2,1,0:T(8,128)(2,1)S(1)} %fusion.21.refs_0_), channel_id=1, source_target_pairs={{0,4},{2,6},{8,0},{10,2},{16,8},{18,10},{24,16},{26,18},{28,24},{3... | collective-permute-start | bytes 1622024 | tf_op jit(solution)/shard_map/ppermute | solution.py:476
  12.2 21.2 %collective-permute-start = (bf16[256,1024]{1,0:T(8,128)(2,1)}, bf16[256,1024]{1,0:T(8,128)(2,1)}, u32[]{:S(2)}, u32[]{:S(2)}) collective-permute-start(bf16[256,1024]{1,0:T(8,128)(2,1)} %fusion.6), channel_id=1, source_target_pairs={{0,1},{1,0},{2,3},{3,2},{4,5},{5,4},{6,7},{7,6},{8,9},{9,8},{10,11... | collective-permute-start | bytes 1572872 | tf_op jit(solution)/shard_map/ppermute | solution.py:555
  15.6 14.2 %collective-permute-start.3 = (bf16[4,64,512]{2,1,0:T(8,128)(2,1)S(1)}, bf16[4,64,512]{2,1,0:T(8,128)(2,1)S(1)}, u32[]{:S(2)}, u32[]{:S(2)}) collective-permute-start(bf16[4,64,512]{2,1,0:T(8,128)(2,1)S(1)} %collective-permute-done.1.refs_1_), channel_id=1, source_target_pairs={{0,8},{2,10},{8,16},{10,18},{16,24},{18,26},{24,28},{26,30},{28,20... | collective-permute-start | bytes 786440 | tf_op jit(solution)/shard_map/ppermute | solution.py:473
  17.2 14.2 %collective-permute-start.4 = (bf16[4,64,512]{2,1,0:T(8,128)(2,1)S(1)}, bf16[4,64,512]{2,1,0:T(8,128)(2,1)S(1)}, u32[]{:S(2)}, u32[]{:S(2)}) collective-permute-start(bf16[4,64,512]{2,1,0:T(8,128)(2,1)S(1)} %collective-permute-done.2.refs_2_), channel_id=1, source_target_pairs={{0,4},{2,6},{8,0},{10,2},{16,8},{18,10},{24,16},{26,18},{28,24},{3... | collective-permute-start | bytes 786440 | tf_op jit(solution)/shard_map/ppermute | solution.py:476
  46.1 14.8 %collective-permute-start.15 = (bf16[3,64,1408]{2,1,0:T(8,128)(2,1)S(1)}, bf16[3,64,1408]{2,1,0:T(8,128)(2,1)}, u32[]{:S(2)}, u32[]{:S(2)}) collective-permute-start(bf16[3,64,1408]{2,1,0:T(8,128)(2,1)S(1)} %copy-done.4), channel_id=1, source_target_pairs={{0,8},{2,10},{8,16},{10,18},{16,24},{18,26},{24,28},{26,30},{28,20... | collective-permute-start | bytes 1622024 | tf_op jit(solution)/shard_map/ppermute | solution.py:473
  47.7 14.4 %collective-permute-start.16 = (bf16[3,64,1408]{2,1,0:T(8,128)(2,1)S(1)}, bf16[3,64,1408]{2,1,0:T(8,128)(2,1)}, u32[]{:S(2)}, u32[]{:S(2)}) collective-permute-start(bf16[3,64,1408]{2,1,0:T(8,128)(2,1)S(1)} %copy-done.7), channel_id=1, source_target_pairs={{0,4},{2,6},{8,0},{10,2},{16,8},{18,10},{24,16},{26,18},{28,24},{3... | collective-permute-start | bytes 1622024 | tf_op jit(solution)/shard_map/ppermute | solution.py:476
  57.9 8.4 %collective-permute-start.13 = (bf16[128,1024]{1,0:T(8,128)(2,1)}, bf16[128,1024]{1,0:T(8,128)(2,1)S(1)}, u32[]{:S(2)}, u32[]{:S(2)}) collective-permute-start(bf16[128,1024]{1,0:T(8,128)(2,1)} %get-tuple-element.81), channel_id=1, source_target_pairs={{0,1},{1,0},{2,3},{3,2},{4,5},{5,4},{6,7},{7,6},{8,9},{9,8},{10,11... | collective-permute-start | bytes 786440 | tf_op jit(solution)/shard_map/ppermute | solution.py:555
  62.2 14.7 %collective-permute-start.17 = (bf16[3,64,1408]{2,1,0:T(8,128)(2,1)}, bf16[3,64,1408]{2,1,0:T(8,128)(2,1)S(1)}, u32[]{:S(2)}, u32[]{:S(2)}) collective-permute-start(bf16[3,64,1408]{2,1,0:T(8,128)(2,1)} %collective-permute-done.15.refs_3_), channel_id=1, source_target_pairs={{0,8},{2,10},{8,16},{10,18},{16,24},{18,26},{24,28},{26,30},{28,20... | collective-permute-start | bytes 1622024 | tf_op jit(solution)/shard_map/ppermute | solution.py:473
  63.7 13.4 %collective-permute-start.18 = (bf16[3,64,1408]{2,1,0:T(8,128)(2,1)}, bf16[3,64,1408]{2,1,0:T(8,128)(2,1)S(1)}, u32[]{:S(2)}, u32[]{:S(2)}) collective-permute-start(bf16[3,64,1408]{2,1,0:T(8,128)(2,1)} %collective-permute-done.16.refs_4_), channel_id=1, source_target_pairs={{0,4},{2,6},{8,0},{10,2},{16,8},{18,10},{24,16},{26,18},{28,24},{3... | collective-permute-start | bytes 1622024 | tf_op jit(solution)/shard_map/ppermute | solution.py:476
  68.8 7.2 %collective-permute-start.14 = (bf16[128,1024]{1,0:T(8,128)(2,1)S(1)}, bf16[128,1024]{1,0:T(8,128)(2,1)S(1)}, u32[]{:S(2)}, u32[]{:S(2)}) collective-permute-start(bf16[128,1024]{1,0:T(8,128)(2,1)S(1)} %fusion.33), channel_id=1, source_target_pairs={{0,1},{1,0},{2,3},{3,2},{4,5},{5,4},{6,7},{7,6},{8,9},{9,8},{10,11... | collective-permute-start | bytes 786440 | tf_op jit(solution)/shard_map/ppermute | solution.py:555
  83.6 9.3 %collective-permute-start.21 = (bf16[3,320,1408]{2,1,0:T(8,128)(2,1)}, bf16[3,320,1408]{2,1,0:T(8,128)(2,1)}, u32[]{:S(2)}, u32[]{:S(2)}) collective-permute-start(bf16[3,320,1408]{2,1,0:T(8,128)(2,1)} %stack_rows.6.refs_0_), channel_id=1, source_target_pairs={{0,2},{2,0},{4,6},{6,4},{8,10},{10,8},{12,14},{14,12},{16,18},{18,... | collective-permute-start | bytes 8110088 | tf_op jit(solution)/shard_map/ppermute | solution.py:479
  109.7 7.7 %collective-permute-start.24 = (bf16[3,512,1408]{2,1,0:T(8,128)(2,1)}, bf16[3,512,1408]{2,1,0:T(8,128)(2,1)}, u32[]{:S(2)}, u32[]{:S(2)}) collective-permute-start(bf16[3,512,1408]{2,1,0:T(8,128)(2,1)} %weight_grads.4), channel_id=1, source_target_pairs={{0,2},{2,0},{4,6},{6,4},{8,10},{10,8},{12,14},{14,12},{16,18},{18,... | collective-permute-start | bytes 12976136 | tf_op jit(solution)/shard_map/ppermute | solution.py:479
  109.8 9.7 %collective-permute-start.23 = (bf16[128,1024]{1,0:T(8,128)(2,1)S(1)}, bf16[128,1024]{1,0:T(8,128)(2,1)S(1)}, u32[]{:S(2)}, u32[]{:S(2)}) collective-permute-start(bf16[128,1024]{1,0:T(8,128)(2,1)S(1)} %copy-done.40), channel_id=1, source_target_pairs={{0,1},{1,0},{2,3},{3,2},{4,5},{5,4},{6,7},{7,6},{8,9},{9,8},{10,11... | collective-permute-start | bytes 786440 | tf_op jit(solution)/shard_map/ppermute | solution.py:555
  121.9 8.3 %collective-permute-start.25 = (bf16[128,1024]{1,0:T(8,128)(2,1)S(1)}, bf16[128,1024]{1,0:T(8,128)(2,1)S(1)}, u32[]{:S(2)}, u32[]{:S(2)}) collective-permute-start(bf16[128,1024]{1,0:T(8,128)(2,1)S(1)} %get-tuple-element.170), channel_id=1, source_target_pairs={{0,1},{1,0},{2,3},{3,2},{4,5},{5,4},{6,7},{7,6},{8,9},{9,8},{10,11... | collective-permute-start | bytes 786440 | tf_op jit(solution)/shard_map/ppermute | solution.py:555
  123.4 8.2 %collective-permute-start.26 = (bf16[3,32,1408]{2,1,0:T(8,128)(2,1)S(1)}, bf16[3,32,1408]{2,1,0:T(8,128)(2,1)S(1)}, u32[]{:S(2)}, u32[]{:S(2)}) collective-permute-start(bf16[3,32,1408]{2,1,0:T(8,128)(2,1)S(1)} %copy-done.36), channel_id=1, source_target_pairs={{0,4},{2,6},{8,0},{10,2},{16,8},{18,10},{24,16},{26,18},{28,24},{3... | collective-permute-start | bytes 811016 | tf_op jit(solution)/shard_map/ppermute | solution.py:476
  124.0 8.0 %collective-permute-start.27 = (bf16[3,32,1408]{2,1,0:T(8,128)(2,1)S(1)}, bf16[3,32,1408]{2,1,0:T(8,128)(2,1)S(1)}, u32[]{:S(2)}, u32[]{:S(2)}) collective-permute-start(bf16[3,32,1408]{2,1,0:T(8,128)(2,1)S(1)} %copy-done.35), channel_id=1, source_target_pairs={{0,8},{2,10},{8,16},{10,18},{16,24},{18,26},{24,28},{26,30},{28,20... | collective-permute-start | bytes 811016 | tf_op jit(solution)/shard_map/ppermute | solution.py:473
  134.6 14.5 %collective-permute-start.30 = (bf16[3,64,1408]{2,1,0:T(8,128)(2,1)}, bf16[3,64,1408]{2,1,0:T(8,128)(2,1)S(1)}, u32[]{:S(2)}, u32[]{:S(2)}) collective-permute-start(bf16[3,64,1408]{2,1,0:T(8,128)(2,1)} %get-tuple-element.100), channel_id=1, source_target_pairs={{0,4},{2,6},{8,0},{10,2},{16,8},{18,10},{24,16},{26,18},{28,24},{3... | collective-permute-start | bytes 1622024 | tf_op jit(solution)/shard_map/ppermute | solution.py:476
  135.1 14.0 %collective-permute-start.31 = (bf16[3,64,1408]{2,1,0:T(8,128)(2,1)}, bf16[3,64,1408]{2,1,0:T(8,128)(2,1)S(1)}, u32[]{:S(2)}, u32[]{:S(2)}) collective-permute-start(bf16[3,64,1408]{2,1,0:T(8,128)(2,1)} %get-tuple-element.101), channel_id=1, source_target_pairs={{0,8},{2,10},{8,16},{10,18},{16,24},{18,26},{24,28},{26,30},{28,20... | collective-permute-start | bytes 1622024 | tf_op jit(solution)/shard_map/ppermute | solution.py:473
  148.3 18.3 %collective-permute-start.28 = (bf16[128,1024]{1,0:T(8,128)(2,1)}, bf16[128,1024]{1,0:T(8,128)(2,1)}, u32[]{:S(2)}, u32[]{:S(2)}) collective-permute-start(bf16[128,1024]{1,0:T(8,128)(2,1)} %get-tuple-element.104), channel_id=1, source_target_pairs={{0,1},{1,0},{2,3},{3,2},{4,5},{5,4},{6,7},{7,6},{8,9},{9,8},{10,11... | collective-permute-start | bytes 786440 | tf_op jit(solution)/shard_map/ppermute | solution.py:555
  151.7 16.4 %collective-permute-start.35 = (bf16[3,64,1408]{2,1,0:T(8,128)(2,1)}, bf16[3,64,1408]{2,1,0:T(8,128)(2,1)}, u32[]{:S(2)}, u32[]{:S(2)}) collective-permute-start(bf16[3,64,1408]{2,1,0:T(8,128)(2,1)} %get-tuple-element.109), channel_id=1, source_target_pairs={{0,4},{2,6},{8,0},{10,2},{16,8},{18,10},{24,16},{26,18},{28,24},{3... | collective-permute-start | bytes 1622024 | tf_op jit(solution)/shard_map/ppermute | solution.py:476
  152.3 15.8 %collective-permute-start.36 = (bf16[3,64,1408]{2,1,0:T(8,128)(2,1)}, bf16[3,64,1408]{2,1,0:T(8,128)(2,1)}, u32[]{:S(2)}, u32[]{:S(2)}) collective-permute-start(bf16[3,64,1408]{2,1,0:T(8,128)(2,1)} %get-tuple-element.110), channel_id=1, source_target_pairs={{0,8},{2,10},{8,16},{10,18},{16,24},{18,26},{24,28},{26,30},{28,20... | collective-permute-start | bytes 1622024 | tf_op jit(solution)/shard_map/ppermute | solution.py:473
  164.6 9.5 %collective-permute-start.33 = (bf16[4,32,512]{2,1,0:T(8,128)(2,1)}, bf16[4,32,512]{2,1,0:T(8,128)(2,1)S(1)}, u32[]{:S(2)}, u32[]{:S(2)}) collective-permute-start(bf16[4,32,512]{2,1,0:T(8,128)(2,1)} %get-tuple-element.115), channel_id=1, source_target_pairs={{0,4},{2,6},{8,0},{10,2},{16,8},{18,10},{24,16},{26,18},{28,24},{3... | collective-permute-start | bytes 393224 | tf_op jit(solution)/shard_map/ppermute | solution.py:476
  165.2 8.9 %collective-permute-start.34 = (bf16[4,32,512]{2,1,0:T(8,128)(2,1)}, bf16[4,32,512]{2,1,0:T(8,128)(2,1)S(1)}, u32[]{:S(2)}, u32[]{:S(2)}) collective-permute-start(bf16[4,32,512]{2,1,0:T(8,128)(2,1)} %get-tuple-element.116), channel_id=1, source_target_pairs={{0,8},{2,10},{8,16},{10,18},{16,24},{18,26},{24,28},{26,30},{28,20... | collective-permute-start | bytes 393224 | tf_op jit(solution)/shard_map/ppermute | solution.py:473
  166.7 18.2 %collective-permute-start.29 = (bf16[128,1024]{1,0:T(8,128)(2,1)S(1)}, bf16[128,1024]{1,0:T(8,128)(2,1)}, u32[]{:S(2)}, u32[]{:S(2)}) collective-permute-start(bf16[128,1024]{1,0:T(8,128)(2,1)S(1)} %copy-done.39), channel_id=1, source_target_pairs={{0,1},{1,0},{2,3},{3,2},{4,5},{5,4},{6,7},{7,6},{8,9},{9,8},{10,11... | collective-permute-start | bytes 786440 | tf_op jit(solution)/shard_map/ppermute | solution.py:555
  172.0 23.9 %collective-permute-start.41 = (bf16[3,64,1408]{2,1,0:T(8,128)(2,1)}, bf16[3,64,1408]{2,1,0:T(8,128)(2,1)S(1)}, u32[]{:S(2)}, u32[]{:S(2)}) collective-permute-start(bf16[3,64,1408]{2,1,0:T(8,128)(2,1)} %get-tuple-element.121), channel_id=1, source_target_pairs={{0,4},{2,6},{8,0},{10,2},{16,8},{18,10},{24,16},{26,18},{28,24},{3... | collective-permute-start | bytes 1622024 | tf_op jit(solution)/shard_map/ppermute | solution.py:476
  172.5 23.4 %collective-permute-start.42 = (bf16[3,64,1408]{2,1,0:T(8,128)(2,1)}, bf16[3,64,1408]{2,1,0:T(8,128)(2,1)}, u32[]{:S(2)}, u32[]{:S(2)}) collective-permute-start(bf16[3,64,1408]{2,1,0:T(8,128)(2,1)} %get-tuple-element.122), channel_id=1, source_target_pairs={{0,8},{2,10},{8,16},{10,18},{16,24},{18,26},{24,28},{26,30},{28,20... | collective-permute-start | bytes 1622024 | tf_op jit(solution)/shard_map/ppermute | solution.py:473
  177.6 14.0 %collective-permute-start.37 = (bf16[4,64,512]{2,1,0:T(8,128)(2,1)}, bf16[4,64,512]{2,1,0:T(8,128)(2,1)S(1)}, u32[]{:S(2)}, u32[]{:S(2)}) collective-permute-start(bf16[4,64,512]{2,1,0:T(8,128)(2,1)} %get-tuple-element.123), channel_id=1, source_target_pairs={{0,4},{2,6},{8,0},{10,2},{16,8},{18,10},{24,16},{26,18},{28,24},{3... | collective-permute-start | bytes 786440 | tf_op jit(solution)/shard_map/ppermute | solution.py:476
  178.1 13.7 %collective-permute-start.38 = (bf16[4,64,512]{2,1,0:T(8,128)(2,1)}, bf16[4,64,512]{2,1,0:T(8,128)(2,1)S(1)}, u32[]{:S(2)}, u32[]{:S(2)}) collective-permute-start(bf16[4,64,512]{2,1,0:T(8,128)(2,1)} %get-tuple-element.124), channel_id=1, source_target_pairs={{0,8},{2,10},{8,16},{10,18},{16,24},{18,26},{24,28},{26,30},{28,20... | collective-permute-start | bytes 786440 | tf_op jit(solution)/shard_map/ppermute | solution.py:473
  193.8 7.0 %collective-permute-start.39 = (bf16[4,64,512]{2,1,0:T(8,128)(2,1)}, bf16[4,64,512]{2,1,0:T(8,128)(2,1)S(1)}, u32[]{:S(2)}, u32[]{:S(2)}) collective-permute-start(bf16[4,64,512]{2,1,0:T(8,128)(2,1)} %get-tuple-element.130), channel_id=1, source_target_pairs={{0,4},{2,6},{8,0},{10,2},{16,8},{18,10},{24,16},{26,18},{28,24},{3... | collective-permute-start | bytes 786440 | tf_op jit(solution)/shard_map/ppermute | solution.py:476
  (56 other events, 278.8 us)
